TPU v7x, 512 devices: a whole 4x4x16 slice. The times are simulated.
512 devices in a mesh: img: 64 (over y, z), lm: 8 (over x, core).
Axes of the slice: x: 4, y: 4, z: 16, core: 2. Of those that a mesh axis runs over, the one named last changes fastest.
Arguments:
- jac_point: float32 [6, 1048576], P(None, ('img', 'lm')), may hold values from -4 to 4
- jac_cam: bfloat16 [1048576, 256], P(('img', 'lm')), may hold values from -0.125 to 0.125
- resid: float32 [2, 1048576], P(None, ('img', 'lm')), may hold values from -6 to 6
- point_ids: int32 [1048576], P(('img', 'lm')), may hold values from 0 to 4095
- cam_ids: int32 [1048576], P(('img', 'lm')), may hold values from 0 to 1023
- owner_slot: int32 [1024], replicated, may hold values from 0 to 1023, each once
- damping: float32 [1], replicated, may hold values from 0.1 to 1
Outputs:
- landmark_step: float32 [3, 32768], P(None, 'lm')
- camera_gradient: float32 [1024, 128], P(('img', 'lm'))
All inputs are finite; a program needn't handle non-finite values.
Results may differ from a plain program's by a relative error of at most 0.0029.
Values sent between devices are 32-bit elements; how exact they have to be, the bound alone decides.
No kernel may reach another device: no remote copies, remote signals or barrier semaphores. Data moves between devices by JAX's collectives and lax.ppermute only.
A program may use at most 64 MiB of HBM per device.

v0:
```python
import jax
import jax.numpy as jnp
from jax import lax
from jax.sharding import PartitionSpec as P

CAMP = 128
BLOCK = 64
LM_BLOCKS = 64


def obs_terms(jac_point, resid):
    u0, u1, u2 = (jac_point[0], jac_point[1], jac_point[2])
    v0, v1, v2 = (jac_point[3], jac_point[4], jac_point[5])
    ru, rv = (resid[0], resid[1])
    return jnp.stack(
        [
            u0 * u0 + v0 * v0,
            u0 * u1 + v0 * v1,
            u0 * u2 + v0 * v2,
            u1 * u1 + v1 * v1,
            u1 * u2 + v1 * v2,
            u2 * u2 + v2 * v2,
            u0 * ru + v0 * rv,
            u1 * ru + v1 * rv,
            u2 * ru + v2 * rv,
        ],
        axis=1,
    )


def solve_points(stats, damping):
    factor = damping[0]
    h01, h02, h12 = (stats[1], stats[2], stats[4])
    a00 = stats[0] + factor * (stats[0] + 1.0)
    a11 = stats[3] + factor * (stats[3] + 1.0)
    a22 = stats[5] + factor * (stats[5] + 1.0)
    g0, g1, g2 = (stats[6], stats[7], stats[8])
    c00 = a11 * a22 - h12 * h12
    c01 = h02 * h12 - h01 * a22
    c02 = h01 * h12 - h02 * a11
    c11 = a00 * a22 - h02 * h02
    c12 = h01 * h02 - a00 * h12
    c22 = a00 * a11 - h01 * h01
    determ = a00 * c00 + h01 * c01 + h02 * c02
    s0 = -(c00 * g0 + c01 * g1 + c02 * g2) / determ
    s1 = -(c01 * g0 + c11 * g1 + c12 * g2) / determ
    s2 = -(c02 * g0 + c12 * g1 + c22 * g2) / determ
    return jnp.stack([s0, s1, s2], axis=0)


def per_device(jac_point, jac_cam, resid, point_ids, cam_ids, owner_slot, damping):
    slice_points = LM_BLOCKS * BLOCK
    terms = obs_terms(jac_point, resid)
    local_stats = jax.ops.segment_sum(terms, point_ids, num_segments=slice_points).T
    stats = lax.psum(local_stats, "img")
    step = solve_points(stats, damping)
    step_obs = jnp.take(step, point_ids, axis=1)
    cu = (
        resid[0]
        + jac_point[0] * step_obs[0]
        + jac_point[1] * step_obs[1]
        + jac_point[2] * step_obs[2]
    )
    cv = (
        resid[1]
        + jac_point[3] * step_obs[0]
        + jac_point[4] * step_obs[1]
        + jac_point[5] * step_obs[2]
    )
    cu_half = cu.astype(jnp.bfloat16)
    cv_half = cv.astype(jnp.bfloat16)
    slots = jnp.take(owner_slot, cam_ids)
    groups_all = owner_slot.shape[0]
    n_obs = cam_ids.shape[0]
    width = min(1024, n_obs)
    group_iota = jnp.arange(groups_all, dtype=jnp.int32)[:, None]
    partial_grad = jnp.zeros((groups_all, CAMP), jnp.float32)
    for block_index in range(n_obs // width):
        lo_row = block_index * width
        block_slots = slots[lo_row : lo_row + width]
        member = (block_slots[None, :] == group_iota).astype(jnp.bfloat16)
        left_u = member * cu_half[None, lo_row : lo_row + width]
        left_v = member * cv_half[None, lo_row : lo_row + width]
        cam_block = jac_cam[lo_row : lo_row + width]
        partial_grad = partial_grad + jnp.dot(
            left_u, cam_block[:, :CAMP], preferred_element_type=jnp.float32
        )
        partial_grad = partial_grad + jnp.dot(
            left_v, cam_block[:, CAMP:], preferred_element_type=jnp.float32
        )
    gradient = lax.psum_scatter(partial_grad, ("img", "lm"), scatter_dimension=0, tiled=True)
    return (step, gradient)


def solution(mesh):
    placed = (
        P(None, ("img", "lm")),
        P(("img", "lm"), None),
        P(None, ("img", "lm")),
        P(("img", "lm")),
        P(("img", "lm")),
        P(),
        P(),
    )
    return jax.shard_map(
        per_device,
        mesh=mesh,
        in_specs=placed,
        out_specs=(P(None, "lm"), P(("img", "lm"), None)),
        check_vma=False,
    )
```

profile of v0, /device:TPU:1, one launch (start us, length us, event | category | flops | bytes accessed | tf_op | source)
XLA Modules:
  0.0 778.2 jit_solution(16912296263779753748)
XLA Ops:
  7.2 0.0 copy-start
  7.2 0.0 all-reduce.4.cloned.1.call-start
  7.2 1.1 add_bitcast_fusion.5
  8.4 1.2 add_bitcast_fusion
  9.5 0.1 stack.4
  9.7 0.4 copy.119
  10.0 0.0 copy-start.5
  10.0 0.0 copy-start.4
  10.0 12.1 %scatter_custom_fusion = f32[4096,9]{1,0:T(8,128)S(1)} fusion(s32[2048]{0:T(1024)} %param.10, f32[2048,9]{1,0:T(8,128)S(1)} %copy.119, f32[]{:T(128)} %constant.30.clone.1), kind=kCustom, calls=%fused_computation.28 | custom fusion | flops 18432 | bytes 147968 | tf_op jit(solution)/shard_map/scatter-add | solution.py:54
  22.1 1.3 copy.120
  23.5 0.0 all-reduce.4.cloned.1.call-update
  23.5 0.0 all-reduce.6.cloned.1.call-start
  23.5 0.0 copy-done.5
  24.2 0.0 copy-done.4
  24.2 0.0 copy-done
  24.2 8.6 %gather_fusion = s32[2048]{0:T(1024)S(1)} fusion(s32[1024]{0:T(1024)S(1)} %copy-done, s32[2048]{0:T(1024)S(1)} %fusion.39), kind=kCustom, calls=%fused_computation | custom fusion | bytes 24576 | tf_op jit(solution)/shard_map/jit(_take)/gather | solution.py:72
  32.8 0.0 copy-start.1
  32.9 0.0 copy-start.3
  32.9 251.7 %all-reduce.4.cloned.1.call-done = f32[9,4096]{1,0:T(8,128)} async-done(((f32[9,4096]{1,0:T(8,128)}), f32[9,4096]{1,0:T(8,128)}) %all-reduce.4.cloned.1.call-update) | async-done | bytes 147472 | tf_op jit(solution)/shard_map/psum | solution.py:55
  284.6 1.7 negate_divide_fusion.2
  286.3 1.8 negate_divide_fusion.1
  288.1 0.0 copy-start.2
  288.2 0.6 copy.121
  288.8 5.5 gather_fusion.1
  294.3 0.3 copy.122
  294.6 0.0 copy-done.1
  294.6 0.0 copy-done.3
  294.7 0.1 add_convert_fusion
  294.7 0.1 slice_reduce_fusion
  294.8 0.0 copy-start.6
  294.8 1.7 fusion.4
  296.5 0.0 copy-done.2
  296.6 0.0 copy-done.6
  296.6 0.7 fusion.22
  297.3 0.7 fusion.19
  298.0 1.5 fusion.16
  299.5 0.0 all-reduce.6.cloned.1.call-update
  299.6 470.5 %all-reduce.6.cloned.1.call-done = f32[1024,128]{1,0:T(8,128)} async-done(((f32[1024,128]{1,0:T(8,128)}), f32[1024,128]{1,0:T(8,128)}) %all-reduce.6.cloned.1.call-update) | async-done | bytes 524304
  770.1 1.2 constant_dynamic-slice_fusion
  (7 shorter events, 0.1 us)
Async XLA Ops:
  7.2 17.1 %copy-start = (s32[1024]{0:T(1024)S(1)}, s32[1024]{0:T(1024)}, u32[]{:S(2)}) copy-start(s32[1024]{0:T(1024)} %param.12) | copy-start | bytes 12292
  7.2 277.4 %all-reduce.4.cloned.1.call-start = ((), (), s32[]{:S(2)}) async-start(), calls=%async_computation | async-start | bytes 524288 | tf_op jit(solution)/shard_map/psum | solution.py:55
  10.0 13.5 %copy-start.5 = (s32[2048]{0:T(1024)S(1)}, s32[2048]{0:T(1024)}, u32[]{:S(2)}) copy-start(s32[2048]{0:T(1024)} %param.10) | copy-start | bytes 24580
  10.0 14.2 %copy-start.4 = (s32[2048]{0:T(1024)S(1)}, s32[2048]{0:T(1024)}, u32[]{:S(2)}) copy-start(s32[2048]{0:T(1024)} %param.11) | copy-start | bytes 24580
  23.5 746.6 %all-reduce.6.cloned.1.call-start = ((), (), s32[]{:S(2)}) async-start(), calls=%async_computation.1 | async-start | bytes 1048576
  32.8 261.8 %copy-start.1 = (f32[6,2048]{1,0:T(8,128)S(1)}, f32[6,2048]{1,0:T(8,128)}, u32[]{:S(2)}) copy-start(f32[6,2048]{1,0:T(8,128)} %param.7) | copy-start | bytes 147460
  32.9 261.8 %copy-start.3 = (f32[2,2048]{1,0:T(2,128)S(1)}, f32[2,2048]{1,0:T(2,128)}, u32[]{:S(2)}) copy-start(f32[2,2048]{1,0:T(2,128)} %param.9) | copy-start | bytes 49156
  288.1 8.4 %copy-start.2 = (f32[3,4096]{1,0:T(4,128)}, f32[3,4096]{1,0:T(4,128)S(1)}, u32[]{:S(2)}) copy-start(f32[3,4096]{1,0:T(4,128)S(1)} %pad_maximum_fusion) | copy-start | bytes 147460
  294.8 1.8 copy-start.6
Sparse Core Ops, SparseCore 0:
  23.6 260.9 all-reduce.3
  299.7 470.3 all-reduce.5
where the time goes:
time: 779 us; the launch traced here: 778 us
  waiting for transfers between devices  722 us (93%)
  local copies, waits for them, and re-layouts  18.2 us (2%)
  other arithmetic  18.1 us (2%)
  between operations  14.9 us (2%)
    unnamed x3, waiting for transfers between devices  471 us
    psum x1, waiting for transfers between devices, per_device(): stats = lax.psum(local_stats, 'img')  252 us
  transfers between devices with their start and end apart: 2, of which 2 were waited for; matrix products, arithmetic and copies ran while one was open for 1% of the time, Pallas kernels for 0%

commit v1 on v0

--- a/solution.py
+++ b/solution.py
@@ -1,6 +1,7 @@
 import jax
 import jax.numpy as jnp
 from jax import lax
+from jax.sharding import Mesh
 from jax.sharding import PartitionSpec as P
 
 CAMP = 128
@@ -48,12 +49,20 @@
     return jnp.stack([s0, s1, s2], axis=0)
 
 
+IMG = ("y", "z")
+LM = ("x", "c")
+ALL = ("y", "z", "x", "c")
+
+
 def per_device(jac_point, jac_cam, resid, point_ids, cam_ids, owner_slot, damping):
     slice_points = LM_BLOCKS * BLOCK
     terms = obs_terms(jac_point, resid)
     local_stats = jax.ops.segment_sum(terms, point_ids, num_segments=slice_points).T
-    stats = lax.psum(local_stats, "img")
-    step = solve_points(stats, damping)
+    parts = local_stats.reshape(9, 64, BLOCK).transpose(1, 0, 2)
+    parts = lax.all_to_all(parts, IMG, 0, 0)
+    own_step = solve_points(jnp.sum(parts, axis=0), damping)
+    steps = lax.all_to_all(jnp.broadcast_to(own_step, (64, 3, BLOCK)), IMG, 0, 0)
+    step = steps.transpose(1, 0, 2).reshape(3, slice_points)
     step_obs = jnp.take(step, point_ids, axis=1)
     cu = (
         resid[0]
@@ -69,7 +78,10 @@
     )
     cu_half = cu.astype(jnp.bfloat16)
     cv_half = cv.astype(jnp.bfloat16)
-    slots = jnp.take(owner_slot, cam_ids)
+    row = owner_slot
+    y, z, x, c, g = row // 256, (row // 16) % 16, (row // 4) % 4, (row // 2) % 2, row % 2
+    place = ((y * 4 + x) * 2 + c) * 32 + z * 2 + g
+    slots = jnp.take(place, cam_ids)
     groups_all = owner_slot.shape[0]
     n_obs = cam_ids.shape[0]
     width = min(1024, n_obs)
@@ -88,24 +100,27 @@
         partial_grad = partial_grad + jnp.dot(
             left_v, cam_block[:, CAMP:], preferred_element_type=jnp.float32
         )
-    gradient = lax.psum_scatter(partial_grad, ("img", "lm"), scatter_dimension=0, tiled=True)
-    return (step, gradient)
+    near = lax.all_to_all(partial_grad.reshape(32, 32, CAMP), ("y", "x", "c"), 0, 0)
+    near = jnp.sum(near, axis=0)
+    far = lax.all_to_all(near.reshape(16, 2, CAMP), "z", 0, 0)
+    return (step, jnp.sum(far, axis=0))
 
 
 def solution(mesh):
+    torus = Mesh(mesh.devices.reshape(4, 16, 4, 2), ALL)
     placed = (
-        P(None, ("img", "lm")),
-        P(("img", "lm"), None),
-        P(None, ("img", "lm")),
-        P(("img", "lm")),
-        P(("img", "lm")),
+        P(None, ALL),
+        P(ALL, None),
+        P(None, ALL),
+        P(ALL),
+        P(ALL),
         P(),
         P(),
     )
     return jax.shard_map(
         per_device,
-        mesh=mesh,
+        mesh=torus,
         in_specs=placed,
-        out_specs=(P(None, "lm"), P(("img", "lm"), None)),
+        out_specs=(P(None, LM), P(ALL, None)),
         check_vma=False,
     )

time: 779 us -> 124 us (0.16)
  waiting for transfers between devices: 722 us -> 29.3 us
  starting transfers between devices: 0.08 us -> 31.7 us
  blocking collectives: 0 us -> 19.5 us
  between operations: 14.9 us -> 1.55 us
    unnamed x3 -> x0, waiting for transfers between devices: 471 us -> none
    psum x1 -> x0, waiting for transfers between devices: 252 us -> none  [per_device(): stats = lax.psum(local_stats, 'img')]
    all_to_all x0 -> x3, starting transfers between devices: none -> 31.7 us  [the longest x1 19.3 us: per_device(): parts = lax.all_to_all(parts, IMG, 0, 0)]
    all_to_all x0 -> x3, waiting for transfers between devices: none -> 29.3 us  [the longest x1 13.5 us: per_device(): lax.all_to_all(jnp.broadcast_to(own_step, (64, 3, BLOCK)), IMG, 0, 0)]
    all_to_all x0 -> x1, blocking collectives: none -> 19.5 us  [per_device(): lax.all_to_all(partial_grad.reshape(32, 32, CAMP), ('y', 'x', 'c'), 0, 0)]
  transfers between devices with their start and end apart: 2 -> 3, of which waited for: 2 -> 3; matrix products, arithmetic and copies ran while one was open for 1% -> 8% of each run, Pallas kernels for 0% -> 0%
where the time goes in v1:
time: 124 us
  starting transfers between devices  31.7 us (26%)
  waiting for transfers between devices  29.3 us (24%)
  local copies, waits for them, and re-layouts  20 us (16%)
  blocking collectives  19.5 us (16%)
  other arithmetic  17.8 us (14%)
  matrix products  3.88 us (3%)
  between operations  1.55 us (1%)
    all_to_all x1, blocking collectives, per_device(): lax.all_to_all(partial_grad.reshape(32, 32, CAMP), ('y', 'x', 'c'), 0, 0)  19.5 us
    all_to_all x1, starting transfers between devices, per_device(): parts = lax.all_to_all(parts, IMG, 0, 0)  19.3 us
    all_to_all x1, waiting for transfers between devices, per_device(): lax.all_to_all(jnp.broadcast_to(own_step, (64, 3, BLOCK)), IMG, 0, 0)  13.5 us
    scatter-add x1, other arithmetic, per_device(): jax.ops.segment_sum(terms, point_ids, num_segments=slice_points)  12.1 us
    all_to_all x1, waiting for transfers between devices, per_device(): far = lax.all_to_all(near.reshape(16, 2, CAMP), 'z', 0, 0)  10 us
    all_to_all x1, starting transfers between devices, per_device(): lax.all_to_all(jnp.broadcast_to(own_step, (64, 3, BLOCK)), IMG, 0, 0)  8.9 us
    gather x1, local copies, waits for them, and re-layouts, per_device(): slots = jnp.take(place, cam_ids)  8.58 us
    all_to_all x1, waiting for transfers between devices, per_device(): parts = lax.all_to_all(parts, IMG, 0, 0)  5.82 us
  transfers between devices with their start and end apart: 3, of which 3 were waited for; matrix products, arithmetic and copies ran while one was open for 8% of the time, Pallas kernels for 0%

profile of v1, /device:TPU:1, one launch (start us, length us, event | category | flops | bytes accessed | tf_op | source)
XLA Modules:
  0.0 123.7 jit_solution(2242326893846101219)
XLA Ops:
  0.6 1.1 add_bitcast_fusion.5
  1.8 1.2 add_bitcast_fusion
  3.0 0.1 stack.4
  3.1 0.4 copy.149
  3.5 12.1 %scatter_custom_fusion = f32[4096,9]{1,0:T(8,128)S(1)} fusion(s32[2048]{0:T(1024)} %param.10, f32[2048,9]{1,0:T(8,128)S(1)} %copy.149, f32[]{:T(128)} %constant.104.clone.1), kind=kCustom, calls=%fused_computation.28 | custom fusion | flops 18432 | bytes 147968 | tf_op jit(solution)/shard_map/scatter-add | solution.py:60
  15.6 0.0 copy-start.2
  15.6 0.0 copy-start.4
  15.6 0.7 copy.151
  16.3 0.9 reshape.405
  17.2 19.3 %all-to-all-start = ((f32[64,1,576]{2,1,0:T(1,128)}), f32[64,1,576]{2,1,0:T(1,128)S(1)}, u32[]{:S(2)}, u32[]{:S(2)}) async-start(f32[64,1,576]{2,1,0:T(1,128)} %reshape.405), calls=%async_computation | async-start | bytes 327680 | tf_op jit(solution)/shard_map/all_to_all | solution.py:62
  37.1 0.0 copy-done.2
  37.2 0.0 copy-done.4
  37.2 0.0 copy-start.3
  37.2 8.6 %gather_fusion = s32[2048]{0:T(1024)S(1)} fusion(s32[1024]{0:T(1024)S(1)} %fusion.48, s32[2048]{0:T(1024)S(1)} %fusion.39), kind=kCustom, calls=%fused_computation | custom fusion | bytes 24576 | tf_op jit(solution)/shard_map/jit(_take)/gather | solution.py:84
  45.8 0.0 copy-done.3
  45.8 5.8 %all-to-all-done = f32[64,1,576]{2,1,0:T(1,128)S(1)} async-done(((f32[64,1,576]{2,1,0:T(1,128)}), f32[64,1,576]{2,1,0:T(1,128)S(1)}, u32[]{:S(2)}, u32[]{:S(2)}) %all-to-all-start) | async-done | bytes 147488 | tf_op jit(solution)/shard_map/all_to_all | solution.py:62
  51.7 0.5 broadcast.149
  52.2 1.0 reduce.8
  53.2 0.1 reshape.406
  53.3 0.1 reduce_sum.27
  53.5 0.8 reshape.407
  54.2 0.0 copy-start
  54.2 0.0 copy-start.1
  54.2 8.9 %all-to-all-start.1 = ((f32[64,1,192]{2,1,0:T(1,128)}), f32[64,1,192]{2,1,0:T(1,128)S(1)}, u32[]{:S(2)}, u32[]{:S(2)}) async-start(f32[64,1,192]{2,1,0:T(1,128)} %reshape.407), calls=%async_computation.1 | async-start | bytes 131072 | tf_op jit(solution)/shard_map/all_to_all | solution.py:64
  63.2 13.5 %all-to-all-done.1 = f32[64,1,192]{2,1,0:T(1,128)S(1)} async-done(((f32[64,1,192]{2,1,0:T(1,128)}), f32[64,1,192]{2,1,0:T(1,128)S(1)}, u32[]{:S(2)}, u32[]{:S(2)}) %all-to-all-start.1) | async-done | bytes 49184 | tf_op jit(solution)/shard_map/all_to_all | solution.py:64
  76.7 0.8 reduce.9
  77.5 0.1 reshape.408
  77.6 0.7 copy.152
  78.3 5.5 %gather_fusion.1 = f32[2048,3]{1,0:T(8,128)S(1)} fusion(f32[3,4096]{0,1:T(8,128)S(1)} %bitcast.33, s32[2048]{0:T(1024)S(1)} %fusion.40), kind=kCustom, calls=%fused_computation.1 | custom fusion | bytes 57344 | tf_op jit(solution)/shard_map/jit(_take)/gather | solution.py:66
  83.7 0.3 copy.153
  84.1 0.0 copy-done
  84.1 0.0 copy-done.1
  84.1 0.1 add_convert_fusion
  84.2 0.1 slice_reduce_fusion
  84.3 0.0 copy-start.5
  84.3 1.7 %fusion.4 = f32[1024,128]{1,0:T(8,128)S(1)} fusion(s32[1024]{0:T(1024)S(1)} %get-tuple-element.36, bf16[1024]{0:T(1024)(128)(2,1)S(1)} %get-tuple-element.37, bf16[2048,256]{1,0:T(8,128)(2,1)} %param.8), kind=kOutput, calls=%fused_computation.9 | convolution fusion | flops 270532608 | bytes 792576 | tf_op jit(solution)/shard_map/dot_general | solution.py:97
  86.0 0.0 copy-done.5
  86.0 0.7 fusion.22
  86.7 0.7 fusion.19
  87.5 0.7 fusion.16
  88.2 19.5 %all_to_all.20 = f32[32,32,128]{2,1,0:T(8,128)S(1)} all-to-all(f32[32,32,128]{2,1,0:T(8,128)S(1)} %bitcast.37), channel_id=1, replica_groups=mesh['y'=4,'z'=16,'x'=4,'c'=2] {'y','x','c'}, dimensions={0} | all-to-all | bytes 1048576 | tf_op jit(solution)/shard_map/all_to_all | solution.py:103
  107.7 0.6 reduce_sum.28
  108.3 3.5 %all-to-all-start.3 = ((f32[16,2,128]{2,1,0:T(2,128)}), f32[16,2,128]{2,1,0:T(2,128)S(1)}, u32[]{:S(2)}, u32[]{:S(2)}) async-start(f32[16,2,128]{2,1,0:T(2,128)} %bitcast.18), calls=%async_computation.3 | async-start | bytes 32768 | tf_op jit(solution)/shard_map/all_to_all | solution.py:105
  111.8 1.2 %copy.155 = f32[3,4096]{1,0:T(4,128)} copy(f32[3,4096]{0,1:T(8,128)S(1)} %bitcast.34) | data formatting | bytes 98304
  113.1 10.0 %all-to-all-done.3 = f32[16,2,128]{2,1,0:T(2,128)S(1)} async-done(((f32[16,2,128]{2,1,0:T(2,128)}), f32[16,2,128]{2,1,0:T(2,128)S(1)}, u32[]{:S(2)}, u32[]{:S(2)}) %all-to-all-start.3) | async-done | bytes 16416 | tf_op jit(solution)/shard_map/all_to_all | solution.py:105
  123.1 0.6 reduce_sum.29
  (11 shorter events, 0.1 us)
Async XLA Ops:
  15.6 21.6 %copy-start.2 = (s32[2048]{0:T(1024)S(1)}, s32[2048]{0:T(1024)}, u32[]{:S(2)}) copy-start(s32[2048]{0:T(1024)} %param.11) | copy-start | bytes 24580
  15.6 21.6 %copy-start.4 = (s32[1024]{0:T(1024)S(1)}, s32[1024]{0:T(1024)}, u32[]{:S(2)}) copy-start(s32[1024]{0:T(1024)} %param.12) | copy-start | bytes 12292
  17.2 34.5 %all-to-all-start = ((f32[64,1,576]{2,1,0:T(1,128)}), f32[64,1,576]{2,1,0:T(1,128)S(1)}, u32[]{:S(2)}, u32[]{:S(2)}) async-start(f32[64,1,576]{2,1,0:T(1,128)} %reshape.405), calls=%async_computation | async-start | bytes 327680 | tf_op jit(solution)/shard_map/all_to_all | solution.py:62
  37.2 8.6 %copy-start.3 = (s32[2048]{0:T(1024)S(1)}, s32[2048]{0:T(1024)}, u32[]{:S(2)}) copy-start(s32[2048]{0:T(1024)} %param.10) | copy-start | bytes 24580
  54.2 29.9 %copy-start = (f32[6,2048]{1,0:T(8,128)S(1)}, f32[6,2048]{1,0:T(8,128)}, u32[]{:S(2)}) copy-start(f32[6,2048]{1,0:T(8,128)} %param.7) | copy-start | bytes 147460
  54.2 29.9 %copy-start.1 = (f32[2,2048]{1,0:T(2,128)S(1)}, f32[2,2048]{1,0:T(2,128)}, u32[]{:S(2)}) copy-start(f32[2,2048]{1,0:T(2,128)} %param.9) | copy-start | bytes 49156
  54.2 22.4 %all-to-all-start.1 = ((f32[64,1,192]{2,1,0:T(1,128)}), f32[64,1,192]{2,1,0:T(1,128)S(1)}, u32[]{:S(2)}, u32[]{:S(2)}) async-start(f32[64,1,192]{2,1,0:T(1,128)} %reshape.407), calls=%async_computation.1 | async-start | bytes 131072 | tf_op jit(solution)/shard_map/all_to_all | solution.py:64
  84.3 1.8 %copy-start.5 = (bf16[2048,256]{1,0:T(8,128)(2,1)S(1)}, bf16[2048,256]{1,0:T(8,128)(2,1)}, u32[]{:S(2)}) copy-start(bf16[2048,256]{1,0:T(8,128)(2,1)} %param.8) | copy-start | bytes 3145732
  108.3 14.8 %all-to-all-start.3 = ((f32[16,2,128]{2,1,0:T(2,128)}), f32[16,2,128]{2,1,0:T(2,128)S(1)}, u32[]{:S(2)}, u32[]{:S(2)}) async-start(f32[16,2,128]{2,1,0:T(2,128)} %bitcast.18), calls=%async_computation.3 | async-start | bytes 32768 | tf_op jit(solution)/shard_map/all_to_all | solution.py:105

commit v2 on v1

v2 whole, which is shorter than its diff:
```python
import jax
import jax.numpy as jnp
from jax import lax
from jax.experimental import pallas as pl
from jax.experimental.pallas import tpu as pltpu
from jax.sharding import Mesh
from jax.sharding import PartitionSpec as P

CAMP = 128
IMG = ("y", "z")
LM = ("x", "c")
ALL = ("y", "z", "x", "c")
NEAR = ("y", "x", "c")
F32 = jnp.float32
BF16 = jnp.bfloat16

LOWS = 16
HIGHS = 256
OWNERS = 64
OWNED = 64
NT = (((1,), (1,)), ((), ()))


def split(value):
    top = value.astype(BF16).astype(F32)
    return top, value - top


def row_of(ref):
    return jnp.concatenate([ref[i : i + 1, :] for i in range(ref.shape[0])], axis=1)


def one_hot(row, count):
    index = lax.broadcasted_iota(jnp.int32, (count, row.shape[1]), 0)
    return jnp.where(index == row, 1.0, 0.0).astype(BF16)


def swap_halves(value):
    return pltpu.roll(value, 64, 1)


def low_lanes(shape):
    return lax.broadcasted_iota(jnp.int32, shape, 1) < 64


def stats_kernel(jac_ref, res_ref, pid_ref, out_ref, hot_ref, terms_ref):
    pid = row_of(pid_ref)
    hot_ref[...] = one_hot(pid & 255, HIGHS)
    low = lax.shift_right_logical(pid, 8)
    u = [jac_ref[a : a + 1, :] for a in range(3)]
    v = [jac_ref[a : a + 1, :] for a in range(3, 6)]
    ru, rv = res_ref[0:1, :], res_ref[1:2, :]
    terms = [u[a] * u[b] + v[a] * v[b] for a, b in ((0, 0), (0, 1), (0, 2), (1, 1), (1, 2), (2, 2))]
    terms += [u[a] * ru + v[a] * rv for a in range(3)]
    member = lax.broadcasted_iota(jnp.int32, (LOWS, pid.shape[1]), 0) == low
    for i, term in enumerate(terms):
        for j, piece in enumerate(split(term)):
            at = (j * 9 + i) * LOWS
            terms_ref[at : at + LOWS, :] = jnp.where(member, piece, 0.0).astype(BF16)
    both = lax.dot_general(terms_ref[...], hot_ref[...], NT, preferred_element_type=F32)
    stats = both[: 9 * LOWS] + both[9 * LOWS :]
    first = low_lanes((LOWS, 128))
    for j in range(5):
        for k in range(4):
            lanes = slice((k // 2) * 128, (k // 2) * 128 + 128)
            one = stats[2 * j * LOWS : (2 * j + 1) * LOWS, lanes]
            if j < 4:
                two = stats[(2 * j + 1) * LOWS : (2 * j + 2) * LOWS, lanes]
            else:
                two = jnp.zeros_like(one)
            if k % 2:
                piece = jnp.where(first, swap_halves(one), two)
            else:
                piece = jnp.where(first, one, swap_halves(two))
            out_ref[k * LOWS : (k + 1) * LOWS, 0, j * 128 : (j + 1) * 128] = piece


def prepare_kernel(pid_ref, cam_ref, slot_ref, jac_ref, hot_ref, place_ref, turned_ref):
    hot_ref[...] = one_hot(row_of(pid_ref) & 255, HIGHS)
    cam = row_of(cam_ref)
    hot = one_hot(cam & 127, 128)
    slot = slot_ref[...]
    y, z, x = slot >> 8, (slot >> 4) & 15, (slot >> 1) & 7
    above, below = y * 8 + x, z * 2 + (slot & 1)
    table = jnp.concatenate([above, below], axis=0).astype(F32).astype(BF16)
    found = jnp.dot(table, hot, preferred_element_type=F32)
    member = lax.broadcasted_iota(jnp.int32, (8, cam.shape[1]), 0) == (cam >> 7)
    places = jnp.where(member, found[:8] * 32.0 + found[8:], 0.0)
    place_ref[...] = jnp.sum(places, axis=0, keepdims=True).astype(jnp.int32)
    turned_ref[...] = jac_ref[...].T


def solve_kernel(damp_ref, parts_ref, out_ref):
    total = parts_ref[0]
    for i in range(1, OWNERS):
        total = total + parts_ref[i]
    s = []
    for v in range(9):
        chunk = total[:, (v // 2) * 128 : (v // 2) * 128 + 128]
        s.append(swap_halves(chunk) if v % 2 else chunk)
    factor = damp_ref[...]
    h01, h02, h12 = s[1], s[2], s[4]
    a00 = s[0] + factor * (s[0] + 1.0)
    a11 = s[3] + factor * (s[3] + 1.0)
    a22 = s[5] + factor * (s[5] + 1.0)
    g0, g1, g2 = s[6], s[7], s[8]
    c00 = a11 * a22 - h12 * h12
    c01 = h02 * h12 - h01 * a22
    c02 = h01 * h12 - h02 * a11
    c11 = a00 * a22 - h02 * h02
    c12 = h01 * h02 - a00 * h12
    c22 = a00 * a11 - h01 * h01
    determ = a00 * c00 + h01 * c01 + h02 * c02
    s0 = -(c00 * g0 + c01 * g1 + c02 * g2) / determ
    s1 = -(c01 * g0 + c11 * g1 + c12 * g2) / determ
    s2 = -(c02 * g0 + c12 * g1 + c22 * g2) / determ
    first = low_lanes((1, 128))
    one = jnp.where(first, s0, swap_halves(s1))
    two = jnp.where(first, s2, 0.0)
    out_ref[...] = jnp.broadcast_to(jnp.concatenate([one, two], axis=1)[None], out_ref.shape)


def camera_kernel(
    steps_ref, jac_ref, res_ref, pid_ref, hot_ref, place_ref, turned_ref, step_ref, grad_ref, right_ref, left_ref
):
    blocks = [steps_ref[k * LOWS : (k + 1) * LOWS, 0, :] for k in range(4)]
    first = low_lanes((LOWS, 128))
    rows = []
    for axis in range(3):
        halves = []
        for kk in range(2):
            at = (axis // 2) * 128
            one, two = blocks[2 * kk][:, at : at + 128], blocks[2 * kk + 1][:, at : at + 128]
            if axis % 2:
                halves.append(jnp.where(first, swap_halves(one), two))
            else:
                halves.append(jnp.where(first, one, swap_halves(two)))
        rows.append(jnp.concatenate(halves, axis=1))
    for axis in range(3):
        for low in range(LOWS):
            step_ref[axis : axis + 1, low * HIGHS : (low + 1) * HIGHS] = rows[axis][low : low + 1, :]
    table = jnp.concatenate(rows, axis=0)
    top, rest = split(table)
    table = jnp.concatenate([top, rest], axis=0).astype(BF16)
    found = jnp.dot(table, hot_ref[...], preferred_element_type=F32)
    found = found[: 3 * LOWS] + found[3 * LOWS :]
    pid = row_of(pid_ref)
    member = lax.broadcasted_iota(jnp.int32, (LOWS, pid.shape[1]), 0) == lax.shift_right_logical(pid, 8)
    s = [
        jnp.sum(jnp.where(member, found[a * LOWS : (a + 1) * LOWS], 0.0), axis=0, keepdims=True)
        for a in range(3)
    ]
    cu = res_ref[0:1, :] + jac_ref[0:1, :] * s[0] + jac_ref[1:2, :] * s[1] + jac_ref[2:3, :] * s[2]
    cv = res_ref[1:2, :] + jac_ref[3:4, :] * s[0] + jac_ref[4:5, :] * s[1] + jac_ref[5:6, :] * s[2]
    cu = cu.astype(BF16).astype(F32)
    cv = cv.astype(BF16).astype(F32)
    terms = turned_ref[:CAMP, :].astype(F32) * cu + turned_ref[CAMP:, :].astype(F32) * cv
    top, rest = split(terms)
    right_ref[:CAMP, :] = top.astype(BF16)
    right_ref[CAMP:, :] = rest.astype(BF16)
    place = place_ref[...]
    for q in range(grad_ref.shape[0] // 256):
        left_ref[...] = one_hot(place - q * 256, 256)
        both = lax.dot_general(left_ref[...], right_ref[...], NT, preferred_element_type=F32)
        grad_ref[q * 256 : (q + 1) * 256, :] = both[:, :CAMP] + both[:, CAMP:]


def shape(dims, kind=F32):
    return jax.ShapeDtypeStruct(dims, kind)


LIMIT = pltpu.CompilerParams(vmem_limit_bytes=16 * 1024 * 1024)


def cost(flops, size):
    return pl.CostEstimate(flops=flops, bytes_accessed=size, transcendentals=0)


def per_device(jac_point, jac_cam, resid, point_ids, cam_ids, owner_slot, damping):
    count = point_ids.shape[0]
    groups = owner_slot.shape[0]
    points = LOWS * HIGHS
    vmem = pl.BlockSpec(memory_space=pltpu.VMEM)
    pids = point_ids.reshape(count // 128, 128)
    cams = cam_ids.reshape(count // 128, 128)
    parts = pl.pallas_call(
        stats_kernel,
        out_shape=shape((OWNERS, 1, 640)),
        in_specs=[vmem] * 3,
        out_specs=vmem,
        scratch_shapes=[pltpu.VMEM((HIGHS, count), BF16), pltpu.VMEM((18 * LOWS, count), BF16)],
        name="stats",
    )(jac_point, resid, pids)
    parts = lax.all_to_all(parts, IMG, 0, 0, tiled=True)
    hot, place, turned = pl.pallas_call(
        prepare_kernel,
        out_shape=(shape((HIGHS, count), BF16), shape((1, count), jnp.int32), shape((2 * CAMP, count), BF16)),
        in_specs=[vmem] * 4,
        out_specs=(vmem, vmem, vmem),
        cost_estimate=cost(10_000_000, 6_000_000),
        compiler_params=LIMIT,
        name="prepare",
    )(pids, cams, owner_slot.reshape(8, groups // 8), jac_cam)
    steps = pl.pallas_call(
        solve_kernel,
        out_shape=shape((OWNERS, 1, 256)),
        in_specs=[vmem, vmem],
        out_specs=vmem,
        compiler_params=LIMIT,
        name="solve",
    )(damping.reshape(1, 1), parts)
    steps = lax.all_to_all(steps, IMG, 0, 0, tiled=True)
    step, partial_grad = pl.pallas_call(
        camera_kernel,
        out_shape=(shape((3, points)), shape((groups, CAMP))),
        in_specs=[vmem] * 7,
        out_specs=(vmem, vmem),
        scratch_shapes=[pltpu.VMEM((2 * CAMP, count), BF16), pltpu.VMEM((256, count), BF16)],
        compiler_params=LIMIT,
        name="camera",
    )(steps, jac_point, resid, pids, hot, place, turned)
    near = lax.all_to_all(partial_grad.reshape(32, 32, CAMP), NEAR, 0, 0, tiled=True)
    near = jnp.sum(near, axis=0)
    far = lax.all_to_all(near.reshape(16, 2, CAMP), "z", 0, 0, tiled=True)
    return (step, jnp.sum(far, axis=0))


def solution(mesh):
    torus = Mesh(mesh.devices.reshape(4, 16, 4, 2), ALL)
    placed = (
        P(None, ALL),
        P(ALL, None),
        P(None, ALL),
        P(ALL),
        P(ALL),
        P(),
        P(),
    )
    return jax.shard_map(
        per_device,
        mesh=torus,
        in_specs=placed,
        out_specs=(P(None, LM), P(ALL, None)),
        check_vma=False,
    )
```

time: 124 us -> 95.7 us (0.77)
  local copies, waits for them, and re-layouts: 20 us -> 1.24 us
  other arithmetic: 17.8 us -> 0.63 us
  blocking collectives: 19.5 us -> 33.4 us
  Pallas kernels: 0 us -> 5.74 us
  starting transfers between devices: 31.7 us -> 26.9 us
  matrix products: 3.88 us -> 0 us
  waiting for transfers between devices: 29.3 us -> 26.1 us
    gather x3 -> x0, local copies, waits for them, and re-layouts: 14.4 us -> none  [the longest x1 8.58 us: per_device(): slots = jnp.take(place, cam_ids)]
    all_to_all x1 -> x2, blocking collectives: 19.5 us -> 33.4 us  [the longest x1 19.6 us: per_device(): lax.all_to_all(partial_grad.reshape(32, 32, CAMP), NEAR, 0, 0, tiled=True)]
    scatter-add x1 -> x0, other arithmetic: 12.1 us -> none  [per_device(): jax.ops.segment_sum(terms, point_ids, num_segments=slice_points)]
    pallas_call x0 -> x4, Pallas kernels: none -> 5.74 us  [the longest x1 2.22 us: per_device(): pl.pallas_call(stats_kernel, out_shape=shape((OWNERS, 1, 640)), in_specs=...]
    all_to_all x3 -> x2, starting transfers between devices: 31.7 us -> 26.9 us  [the longest x1 19.3 us: per_device(): parts = lax.all_to_all(parts, IMG, 0, 0, tiled=True)]
    dot_general x4 -> x0, matrix products: 3.88 us -> none  [the longest x2 2.46 us: per_device(): jnp.dot(left_u, cam_block[:, :CAMP], preferred_element_type=jnp.float32)]
    all_to_all x3 -> x2, waiting for transfers between devices: 29.3 us -> 26.1 us  [the longest x1 14.5 us: per_device(): parts = lax.all_to_all(parts, IMG, 0, 0, tiled=True)]
    add x3 -> x0, other arithmetic: 2.36 us -> none  [the longest x1 1.2 us: obs_terms(): u2 * ru + v2 * rv]
  transfers between devices with their start and end apart: 3 -> 2, of which waited for: 3 -> 2; matrix products, arithmetic and copies ran while one was open for 8% -> 0% of each run, Pallas kernels for 0% -> 1%
where the time goes in v2:
time: 95.7 us; the launch traced here: 95.3 us
  blocking collectives  33.4 us (35%)
  starting transfers between devices  26.9 us (28%)
  waiting for transfers between devices  26.1 us (27%)
  Pallas kernels  5.74 us (6%)
  between operations  1.34 us (1%)
  local copies, waits for them, and re-layouts  1.24 us (1%)
    all_to_all x1, blocking collectives, per_device(): lax.all_to_all(partial_grad.reshape(32, 32, CAMP), NEAR, 0, 0, tiled=True)  19.6 us
    all_to_all x1, starting transfers between devices, per_device(): parts = lax.all_to_all(parts, IMG, 0, 0, tiled=True)  19.3 us
    all_to_all x1, waiting for transfers between devices, per_device(): parts = lax.all_to_all(parts, IMG, 0, 0, tiled=True)  14.5 us
    all_to_all x1, blocking collectives, per_device(): far = lax.all_to_all(near.reshape(16, 2, CAMP), 'z', 0, 0, tiled=True)  13.9 us
    all_to_all x1, waiting for transfers between devices, per_device(): steps = lax.all_to_all(steps, IMG, 0, 0, tiled=True)  11.6 us
    all_to_all x1, starting transfers between devices, per_device(): steps = lax.all_to_all(steps, IMG, 0, 0, tiled=True)  7.59 us
    pallas_call x1, Pallas kernels, per_device(): pl.pallas_call(stats_kernel, out_shape=shape((OWNERS, 1, 640)), in_specs=...  2.22 us
    pallas_call x1, Pallas kernels, per_device(): pl.pallas_call(camera_kernel, out_shape=(shape((3, points)), shape((group...  1.93 us
  transfers between devices with their start and end apart: 2, of which 2 were waited for; matrix products, arithmetic and copies ran while one was open for 0% of the time, Pallas kernels for 1%

profile of v2, /device:TPU:1, one launch (start us, length us, event | category | flops | bytes accessed | tf_op | source)
XLA Modules:
  0.0 95.3 jit_solution(9635931860284256072)
XLA Ops:
  0.6 2.2 %stats.1 = f32[64,1,640]{2,1,0:T(1,128)} custom-call(f32[6,2048]{1,0:T(8,128)} %jac_ref.5, f32[2,2048]{1,0:T(2,128)} %res_ref.3, s32[16,128]{1,0:T(8,128)} %bitcast.8), custom_call_target="tpu_custom_call" | custom-call | tf_op jit(solution)/shard_map/stats/pallas_call | solution.py:186
  2.8 19.3 %all-to-all-start = ((f32[64,1,640]{2,1,0:T(1,128)}), f32[64,1,640]{2,1,0:T(1,128)S(1)}, u32[]{:S(2)}, u32[]{:S(2)}) async-start(f32[64,1,640]{2,1,0:T(1,128)} %stats.1), calls=%async_computation | async-start | bytes 327680 | tf_op jit(solution)/shard_map/all_to_all | solution.py:194
  22.8 14.5 %all-to-all-done.parts_ref = f32[64,1,640]{2,1,0:T(1,128)S(1)} async-done(((f32[64,1,640]{2,1,0:T(1,128)}), f32[64,1,640]{2,1,0:T(1,128)S(1)}, u32[]{:S(2)}, u32[]{:S(2)}) %all-to-all-start) | async-done | bytes 163872 | tf_op jit(solution)/shard_map/all_to_all | solution.py:194
  37.3 0.9 solve.1
  38.2 0.0 copy-start.2
  38.2 0.0 copy-start.4
  38.2 0.0 copy-start.5
  38.2 7.6 %all-to-all-start.1 = ((f32[64,1,256]{2,1,0:T(1,128)}), f32[64,1,256]{2,1,0:T(1,128)S(1)}, u32[]{:S(2)}, u32[]{:S(2)}) async-start(f32[64,1,256]{2,1,0:T(1,128)} %solve.1), calls=%async_computation.1 | async-start | bytes 131072 | tf_op jit(solution)/shard_map/all_to_all | solution.py:212
  45.8 0.0 copy-done.2
  45.8 0.0 copy-done.4
  45.8 0.0 copy-done.5
  45.8 0.0 copy-start
  45.8 1.2 %copy-done = bf16[2048,256]{1,0:T(8,128)(2,1)S(1)} copy-done((bf16[2048,256]{1,0:T(8,128)(2,1)S(1)}, bf16[2048,256]{1,0:T(8,128)(2,1)}, u32[]{:S(2)}) %copy-start) | copy-done | bytes 1048600
  47.0 0.0 copy-start.1
  47.0 0.0 copy-start.3
  47.0 0.7 prepare.1
  47.8 11.6 %all-to-all-done.1.steps_ref = f32[64,1,256]{2,1,0:T(1,128)S(1)} async-done(((f32[64,1,256]{2,1,0:T(1,128)}), f32[64,1,256]{2,1,0:T(1,128)S(1)}, u32[]{:S(2)}, u32[]{:S(2)}) %all-to-all-start.1) | async-done | bytes 65568 | tf_op jit(solution)/shard_map/all_to_all | solution.py:212
  59.3 0.0 copy-done.1
  59.3 0.0 copy-done.3
  59.3 1.9 %camera.1 = (f32[3,4096]{1,0:T(4,128)}, f32[1024,128]{1,0:T(8,128)S(1)}) custom-call(f32[64,1,256]{2,1,0:T(1,128)S(1)} %all-to-all-done.1.steps_ref, f32[6,2048]{1,0:T(8,128)S(1)} %copy-done.1, f32[2,2048]{1,0:T(2,128)S(1)} %copy-done.3, s32[16,128]{1,0:T(8,128)S(1)} %bitcast.10, bf16[256,2048]{1,0:T(8,128)(2,1)S(1)} %get-tuple-element.7.hot_ref, ...), custom_call_target="tpu_custom_call" | custom-call | tf_op jit(solution)/shard_map/camera/pallas_call | solution.py:213
  61.3 19.6 %all_to_all.20 = f32[32,32,128]{2,1,0:T(8,128)S(1)} all-to-all(f32[32,32,128]{2,1,0:T(8,128)S(1)} %bitcast.7), channel_id=1, replica_groups=mesh['y'=4,'z'=16,'x'=4,'c'=2] {'y','x','c'}, dimensions={0} | all-to-all | bytes 1048576 | tf_op jit(solution)/shard_map/all_to_all | solution.py:222
  80.9 13.9 %all_to_all.21 = f32[16,2,128]{2,1,0:T(2,128)S(1)} all-to-all(f32[16,2,128]{2,1,0:T(2,128)S(1)} %bitcast.13), channel_id=1, replica_groups=mesh['y'=4,'z'=16,'x'=4,'c'=2] {'z'}, dimensions={0} | all-to-all | bytes 32768 | tf_op jit(solution)/shard_map/all_to_all | solution.py:224
  94.8 0.6 reduce_sum.19
  (1 shorter events, 0.0 us)
Async XLA Ops:
  2.8 34.5 %all-to-all-start = ((f32[64,1,640]{2,1,0:T(1,128)}), f32[64,1,640]{2,1,0:T(1,128)S(1)}, u32[]{:S(2)}, u32[]{:S(2)}) async-start(f32[64,1,640]{2,1,0:T(1,128)} %stats.1), calls=%async_computation | async-start | bytes 327680 | tf_op jit(solution)/shard_map/all_to_all | solution.py:194
  38.2 7.6 %copy-start.2 = (s32[2048]{0:T(1024)S(1)}, s32[2048]{0:T(1024)}, u32[]{:S(2)}) copy-start(s32[2048]{0:T(1024)} %param.10) | copy-start | bytes 24580
  38.2 7.6 %copy-start.4 = (s32[2048]{0:T(1024)S(1)}, s32[2048]{0:T(1024)}, u32[]{:S(2)}) copy-start(s32[2048]{0:T(1024)} %param.11) | copy-start | bytes 24580
  38.2 7.6 %copy-start.5 = (s32[1024]{0:T(1024)S(1)}, s32[1024]{0:T(1024)}, u32[]{:S(2)}) copy-start(s32[1024]{0:T(1024)} %param.12) | copy-start | bytes 12292
  38.2 21.2 %all-to-all-start.1 = ((f32[64,1,256]{2,1,0:T(1,128)}), f32[64,1,256]{2,1,0:T(1,128)S(1)}, u32[]{:S(2)}, u32[]{:S(2)}) async-start(f32[64,1,256]{2,1,0:T(1,128)} %solve.1), calls=%async_computation.1 | async-start | bytes 131072 | tf_op jit(solution)/shard_map/all_to_all | solution.py:212
  45.8 1.2 %copy-start = (bf16[2048,256]{1,0:T(8,128)(2,1)S(1)}, bf16[2048,256]{1,0:T(8,128)(2,1)}, u32[]{:S(2)}) copy-start(bf16[2048,256]{1,0:T(8,128)(2,1)} %jac_ref.4) | copy-start | bytes 3145732
  47.0 12.3 %copy-start.1 = (f32[6,2048]{1,0:T(8,128)S(1)}, f32[6,2048]{1,0:T(8,128)}, u32[]{:S(2)}) copy-start(f32[6,2048]{1,0:T(8,128)} %jac_ref.5) | copy-start | bytes 147460
  47.0 12.3 %copy-start.3 = (f32[2,2048]{1,0:T(2,128)S(1)}, f32[2,2048]{1,0:T(2,128)}, u32[]{:S(2)}) copy-start(f32[2,2048]{1,0:T(2,128)} %res_ref.3) | copy-start | bytes 49156

commit v3 on v2

--- a/solution.py
+++ b/solution.py
@@ -1,5 +1,6 @@
 import jax
 import jax.numpy as jnp
+import numpy as np
 from jax import lax
 from jax.experimental import pallas as pl
 from jax.experimental.pallas import tpu as pltpu
@@ -10,7 +11,12 @@
 IMG = ("y", "z")
 LM = ("x", "c")
 ALL = ("y", "z", "x", "c")
-NEAR = ("y", "x", "c")
+FLAT = ("img", "lm")
+GRID = np.arange(512).reshape(4, 16, 4, 2)
+TURNED = GRID[[2, 3, 0, 1]][:, [z ^ 8 for z in range(16)]][:, :, [2, 3, 0, 1]]
+IMG_GROUPS = [TURNED[:, :, x, c].reshape(-1).tolist() for x in range(4) for c in range(2)]
+NEAR_GROUPS = [TURNED[:, z].reshape(-1).tolist() for z in range(16)]
+FAR_GROUPS = [TURNED[y, :, x, c].tolist() for y in range(4) for x in range(4) for c in range(2)]
 F32 = jnp.float32
 BF16 = jnp.bfloat16
 
@@ -80,7 +86,7 @@
     cam = row_of(cam_ref)
     hot = one_hot(cam & 127, 128)
     slot = slot_ref[...]
-    y, z, x = slot >> 8, (slot >> 4) & 15, (slot >> 1) & 7
+    y, z, x = (slot >> 8) ^ 2, ((slot >> 4) & 15) ^ 8, ((slot >> 1) & 7) ^ 4
     above, below = y * 8 + x, z * 2 + (slot & 1)
     table = jnp.concatenate([above, below], axis=0).astype(F32).astype(BF16)
     found = jnp.dot(table, hot, preferred_element_type=F32)
@@ -176,6 +182,10 @@
     return pl.CostEstimate(flops=flops, bytes_accessed=size, transcendentals=0)
 
 
+def exchange(value, groups):
+    return lax.all_to_all(value, FLAT, 0, 0, axis_index_groups=groups, tiled=True)
+
+
 def per_device(jac_point, jac_cam, resid, point_ids, cam_ids, owner_slot, damping):
     count = point_ids.shape[0]
     groups = owner_slot.shape[0]
@@ -191,7 +201,7 @@
         scratch_shapes=[pltpu.VMEM((HIGHS, count), BF16), pltpu.VMEM((18 * LOWS, count), BF16)],
         name="stats",
     )(jac_point, resid, pids)
-    parts = lax.all_to_all(parts, IMG, 0, 0, tiled=True)
+    parts = exchange(parts, IMG_GROUPS)
     hot, place, turned = pl.pallas_call(
         prepare_kernel,
         out_shape=(shape((HIGHS, count), BF16), shape((1, count), jnp.int32), shape((2 * CAMP, count), BF16)),
@@ -209,7 +219,7 @@
         compiler_params=LIMIT,
         name="solve",
     )(damping.reshape(1, 1), parts)
-    steps = lax.all_to_all(steps, IMG, 0, 0, tiled=True)
+    steps = exchange(steps, IMG_GROUPS)
     step, partial_grad = pl.pallas_call(
         camera_kernel,
         out_shape=(shape((3, points)), shape((groups, CAMP))),
@@ -219,27 +229,18 @@
         compiler_params=LIMIT,
         name="camera",
     )(steps, jac_point, resid, pids, hot, place, turned)
-    near = lax.all_to_all(partial_grad.reshape(32, 32, CAMP), NEAR, 0, 0, tiled=True)
+    near = exchange(partial_grad.reshape(32, 32, CAMP), NEAR_GROUPS)
     near = jnp.sum(near, axis=0)
-    far = lax.all_to_all(near.reshape(16, 2, CAMP), "z", 0, 0, tiled=True)
+    far = exchange(near.reshape(16, 2, CAMP), FAR_GROUPS)
     return (step, jnp.sum(far, axis=0))
 
 
 def solution(mesh):
-    torus = Mesh(mesh.devices.reshape(4, 16, 4, 2), ALL)
-    placed = (
-        P(None, ALL),
-        P(ALL, None),
-        P(None, ALL),
-        P(ALL),
-        P(ALL),
-        P(),
-        P(),
-    )
+    placed = (P(None, FLAT), P(FLAT, None), P(None, FLAT), P(FLAT), P(FLAT), P(), P())
     return jax.shard_map(
         per_device,
-        mesh=torus,
+        mesh=mesh,
         in_specs=placed,
-        out_specs=(P(None, LM), P(ALL, None)),
+        out_specs=(P(None, "lm"), P(FLAT, None)),
         check_vma=False,
     )

time: 95.7 us -> 86.6 us (0.905)
  waiting for transfers between devices: 26.1 us -> 7.19 us
  starting transfers between devices: 26.9 us -> 38.6 us
  blocking collectives: 33.4 us -> 31.5 us
    all_to_all x2, waiting for transfers between devices: 26.1 us -> 7.19 us  [exchange(): lax.all_to_all(value, FLAT, 0, 0, axis_index_groups=groups, tiled=True)]
    all_to_all x2, starting transfers between devices: 26.9 us -> 38.6 us  [exchange(): lax.all_to_all(value, FLAT, 0, 0, axis_index_groups=groups, tiled=True)]
    all_to_all x2, blocking collectives: 33.4 us -> 31.5 us  [exchange(): lax.all_to_all(value, FLAT, 0, 0, axis_index_groups=groups, tiled=True)]
where the time goes in v3:
time: 86.6 us; the launch traced here: 86.2 us
  starting transfers between devices  38.6 us (45%)
  blocking collectives  31.5 us (36%)
  waiting for transfers between devices  7.19 us (8%)
  Pallas kernels  5.74 us (7%)
  between operations  1.34 us (2%)
  local copies, waits for them, and re-layouts  1.24 us (1%)
    all_to_all x2, starting transfers between devices, exchange(): lax.all_to_all(value, FLAT, 0, 0, axis_index_groups=groups, tiled=True)  38.6 us
    all_to_all x2, blocking collectives, exchange(): lax.all_to_all(value, FLAT, 0, 0, axis_index_groups=groups, tiled=True)  31.5 us
    all_to_all x2, waiting for transfers between devices, exchange(): lax.all_to_all(value, FLAT, 0, 0, axis_index_groups=groups, tiled=True)  7.19 us
    pallas_call x1, Pallas kernels, per_device(): pl.pallas_call(stats_kernel, out_shape=shape((OWNERS, 1, 640)), in_specs=...  2.22 us
    pallas_call x1, Pallas kernels, per_device(): pl.pallas_call(camera_kernel, out_shape=(shape((3, points)), shape((group...  1.93 us
  transfers between devices with their start and end apart: 2, of which 2 were waited for; matrix products, arithmetic and copies ran while one was open for 0% of the time, Pallas kernels for 1%

profile of v3, /device:TPU:1, one launch (start us, length us, event | category | flops | bytes accessed | tf_op | source)
XLA Modules:
  0.0 86.2 jit_solution(10796361410357815264)
XLA Ops:
  0.6 2.2 %stats.1 = f32[64,1,640]{2,1,0:T(1,128)} custom-call(f32[6,2048]{1,0:T(8,128)} %jac_ref.5, f32[2,2048]{1,0:T(2,128)} %res_ref.3, s32[16,128]{1,0:T(8,128)} %bitcast.8), custom_call_target="tpu_custom_call" | custom-call | tf_op jit(solution)/shard_map/stats/pallas_call | solution.py:196
  2.8 23.2 %all-to-all-start = ((f32[64,1,640]{2,1,0:T(1,128)}), f32[64,1,640]{2,1,0:T(1,128)S(1)}, u32[]{:S(2)}, u32[]{:S(2)}) async-start(f32[64,1,640]{2,1,0:T(1,128)} %stats.1), calls=%async_computation | async-start | bytes 327680 | tf_op jit(solution)/shard_map/all_to_all | solution.py:186
  26.7 6.6 %all-to-all-done.parts_ref = f32[64,1,640]{2,1,0:T(1,128)S(1)} async-done(((f32[64,1,640]{2,1,0:T(1,128)}), f32[64,1,640]{2,1,0:T(1,128)S(1)}, u32[]{:S(2)}, u32[]{:S(2)}) %all-to-all-start) | async-done | bytes 163872 | tf_op jit(solution)/shard_map/all_to_all | solution.py:186
  33.2 0.9 %solve.1 = f32[64,1,256]{2,1,0:T(1,128)} custom-call(f32[1,1]{1,0:T(1,128)} %bitcast.6.damp_ref, f32[64,1,640]{2,1,0:T(1,128)S(1)} %all-to-all-done.parts_ref), custom_call_target="tpu_custom_call" | custom-call | tf_op jit(solution)/shard_map/solve/pallas_call | solution.py:214
  34.1 0.0 copy-start.2
  34.1 0.0 copy-start.4
  34.1 0.0 copy-start.5
  34.1 15.4 %all-to-all-start.1 = ((f32[64,1,256]{2,1,0:T(1,128)}), f32[64,1,256]{2,1,0:T(1,128)S(1)}, u32[]{:S(2)}, u32[]{:S(2)}) async-start(f32[64,1,256]{2,1,0:T(1,128)} %solve.1), calls=%async_computation.1 | async-start | bytes 131072 | tf_op jit(solution)/shard_map/all_to_all | solution.py:186
  49.6 0.0 copy-done.2
  49.6 0.0 copy-done.4
  49.6 0.0 copy-done.5
  49.6 0.0 copy-start
  49.6 1.2 %copy-done = bf16[2048,256]{1,0:T(8,128)(2,1)S(1)} copy-done((bf16[2048,256]{1,0:T(8,128)(2,1)S(1)}, bf16[2048,256]{1,0:T(8,128)(2,1)}, u32[]{:S(2)}) %copy-start) | copy-done | bytes 1048600
  50.8 0.0 copy-start.1
  50.8 0.0 copy-start.3
  50.8 0.7 prepare.1
  51.5 0.6 all-to-all-done.1.steps_ref
  52.2 0.0 copy-done.1
  52.2 0.0 copy-done.3
  52.2 1.9 %camera.1 = (f32[3,4096]{1,0:T(4,128)}, f32[1024,128]{1,0:T(8,128)S(1)}) custom-call(f32[64,1,256]{2,1,0:T(1,128)S(1)} %all-to-all-done.1.steps_ref, f32[6,2048]{1,0:T(8,128)S(1)} %copy-done.1, f32[2,2048]{1,0:T(2,128)S(1)} %copy-done.3, s32[16,128]{1,0:T(8,128)S(1)} %bitcast.10, bf16[256,2048]{1,0:T(8,128)(2,1)S(1)} %get-tuple-element.7.hot_ref, ...), custom_call_target="tpu_custom_call" | custom-call | tf_op jit(solution)/shard_map/camera/pallas_call | solution.py:223
  54.1 17.6 %all_to_all.20 = f32[32,32,128]{2,1,0:T(8,128)S(1)} all-to-all(f32[32,32,128]{2,1,0:T(8,128)S(1)} %bitcast.7), channel_id=1, replica_groups={{324,325,326,327,320,321,322,323,452,453,454,455,448,449,450,451,68,69,..., dimensions={0} | all-to-all | bytes 1048576 | tf_op jit(solution)/shard_map/all_to_all | solution.py:186
  71.8 13.8 %all_to_all.21 = f32[16,2,128]{2,1,0:T(2,128)S(1)} all-to-all(f32[16,2,128]{2,1,0:T(2,128)S(1)} %bitcast.13), channel_id=1, replica_groups={{324,332,340,348,356,364,372,380,260,268,276,284,292,300,308,316},{325,..., dimensions={0} | all-to-all | bytes 32768 | tf_op jit(solution)/shard_map/all_to_all | solution.py:186
  85.6 0.6 reduce_sum.19
  (1 shorter events, 0.0 us)
Async XLA Ops:
  2.8 30.4 %all-to-all-start = ((f32[64,1,640]{2,1,0:T(1,128)}), f32[64,1,640]{2,1,0:T(1,128)S(1)}, u32[]{:S(2)}, u32[]{:S(2)}) async-start(f32[64,1,640]{2,1,0:T(1,128)} %stats.1), calls=%async_computation | async-start | bytes 327680 | tf_op jit(solution)/shard_map/all_to_all | solution.py:186
  34.1 15.5 %copy-start.2 = (s32[2048]{0:T(1024)S(1)}, s32[2048]{0:T(1024)}, u32[]{:S(2)}) copy-start(s32[2048]{0:T(1024)} %param.10) | copy-start | bytes 24580
  34.1 15.5 %copy-start.4 = (s32[2048]{0:T(1024)S(1)}, s32[2048]{0:T(1024)}, u32[]{:S(2)}) copy-start(s32[2048]{0:T(1024)} %param.11) | copy-start | bytes 24580
  34.1 15.5 %copy-start.5 = (s32[1024]{0:T(1024)S(1)}, s32[1024]{0:T(1024)}, u32[]{:S(2)}) copy-start(s32[1024]{0:T(1024)} %param.12) | copy-start | bytes 12292
  34.1 18.0 %all-to-all-start.1 = ((f32[64,1,256]{2,1,0:T(1,128)}), f32[64,1,256]{2,1,0:T(1,128)S(1)}, u32[]{:S(2)}, u32[]{:S(2)}) async-start(f32[64,1,256]{2,1,0:T(1,128)} %solve.1), calls=%async_computation.1 | async-start | bytes 131072 | tf_op jit(solution)/shard_map/all_to_all | solution.py:186
  49.6 1.2 %copy-start = (bf16[2048,256]{1,0:T(8,128)(2,1)S(1)}, bf16[2048,256]{1,0:T(8,128)(2,1)}, u32[]{:S(2)}) copy-start(bf16[2048,256]{1,0:T(8,128)(2,1)} %jac_ref.4) | copy-start | bytes 3145732
  50.8 1.3 %copy-start.1 = (f32[6,2048]{1,0:T(8,128)S(1)}, f32[6,2048]{1,0:T(8,128)}, u32[]{:S(2)}) copy-start(f32[6,2048]{1,0:T(8,128)} %jac_ref.5) | copy-start | bytes 147460
  50.8 1.3 %copy-start.3 = (f32[2,2048]{1,0:T(2,128)S(1)}, f32[2,2048]{1,0:T(2,128)}, u32[]{:S(2)}) copy-start(f32[2,2048]{1,0:T(2,128)} %res_ref.3) | copy-start | bytes 49156

commit v4 on v3

--- a/solution.py
+++ b/solution.py
@@ -14,7 +14,9 @@
 FLAT = ("img", "lm")
 GRID = np.arange(512).reshape(4, 16, 4, 2)
 TURNED = GRID[[2, 3, 0, 1]][:, [z ^ 8 for z in range(16)]][:, :, [2, 3, 0, 1]]
-IMG_GROUPS = [TURNED[:, :, x, c].reshape(-1).tolist() for x in range(4) for c in range(2)]
+PAIRS = TURNED.reshape(4, 8, 2, 4, 2)
+CLOSE_GROUPS = [PAIRS[:, z, :, x, c].reshape(-1).tolist() for z in range(8) for x in range(4) for c in range(2)]
+LINE_GROUPS = [PAIRS[y, :, z, x, c].tolist() for y in range(4) for z in range(2) for x in range(4) for c in range(2)]
 NEAR_GROUPS = [TURNED[:, z].reshape(-1).tolist() for z in range(16)]
 FAR_GROUPS = [TURNED[y, :, x, c].tolist() for y in range(4) for x in range(4) for c in range(2)]
 F32 = jnp.float32
@@ -22,8 +24,8 @@
 
 LOWS = 16
 HIGHS = 256
-OWNERS = 64
-OWNED = 64
+OWNERS = 8
+OWNED = 512
 NT = (((1,), (1,)), ((), ()))
 
 
@@ -39,14 +41,6 @@
 def one_hot(row, count):
     index = lax.broadcasted_iota(jnp.int32, (count, row.shape[1]), 0)
     return jnp.where(index == row, 1.0, 0.0).astype(BF16)
-
-
-def swap_halves(value):
-    return pltpu.roll(value, 64, 1)
-
-
-def low_lanes(shape):
-    return lax.broadcasted_iota(jnp.int32, shape, 1) < 64
 
 
 def stats_kernel(jac_ref, res_ref, pid_ref, out_ref, hot_ref, terms_ref):
@@ -65,20 +59,11 @@
             terms_ref[at : at + LOWS, :] = jnp.where(member, piece, 0.0).astype(BF16)
     both = lax.dot_general(terms_ref[...], hot_ref[...], NT, preferred_element_type=F32)
     stats = both[: 9 * LOWS] + both[9 * LOWS :]
-    first = low_lanes((LOWS, 128))
-    for j in range(5):
-        for k in range(4):
-            lanes = slice((k // 2) * 128, (k // 2) * 128 + 128)
-            one = stats[2 * j * LOWS : (2 * j + 1) * LOWS, lanes]
-            if j < 4:
-                two = stats[(2 * j + 1) * LOWS : (2 * j + 2) * LOWS, lanes]
-            else:
-                two = jnp.zeros_like(one)
-            if k % 2:
-                piece = jnp.where(first, swap_halves(one), two)
-            else:
-                piece = jnp.where(first, one, swap_halves(two))
-            out_ref[k * LOWS : (k + 1) * LOWS, 0, j * 128 : (j + 1) * 128] = piece
+    for v in range(9):
+        for low in range(LOWS):
+            at = v * OWNED + (low % 2) * HIGHS
+            row = v * LOWS + low
+            out_ref[low // 2, :, at : at + HIGHS] = stats[row : row + 1, :]
 
 
 def prepare_kernel(pid_ref, cam_ref, slot_ref, jac_ref, hot_ref, place_ref, turned_ref):
@@ -96,14 +81,20 @@
     turned_ref[...] = jac_ref[...].T
 
 
-def solve_kernel(damp_ref, parts_ref, out_ref):
+def total_of(parts_ref):
     total = parts_ref[0]
     for i in range(1, OWNERS):
         total = total + parts_ref[i]
-    s = []
-    for v in range(9):
-        chunk = total[:, (v // 2) * 128 : (v // 2) * 128 + 128]
-        s.append(swap_halves(chunk) if v % 2 else chunk)
+    return total
+
+
+def gather_kernel(parts_ref, out_ref):
+    out_ref[...] = jnp.broadcast_to(total_of(parts_ref)[None], out_ref.shape)
+
+
+def solve_kernel(damp_ref, parts_ref, out_ref):
+    total = total_of(parts_ref)
+    s = [total[:, v * OWNED : (v + 1) * OWNED] for v in range(9)]
     factor = damp_ref[...]
     h01, h02, h12 = s[1], s[2], s[4]
     a00 = s[0] + factor * (s[0] + 1.0)
@@ -120,32 +111,19 @@
     s0 = -(c00 * g0 + c01 * g1 + c02 * g2) / determ
     s1 = -(c01 * g0 + c11 * g1 + c12 * g2) / determ
     s2 = -(c02 * g0 + c12 * g1 + c22 * g2) / determ
-    first = low_lanes((1, 128))
-    one = jnp.where(first, s0, swap_halves(s1))
-    two = jnp.where(first, s2, 0.0)
-    out_ref[...] = jnp.broadcast_to(jnp.concatenate([one, two], axis=1)[None], out_ref.shape)
+    out_ref[...] = jnp.broadcast_to(jnp.concatenate([s0, s1, s2], axis=1)[None], out_ref.shape)
 
 
 def camera_kernel(
-    steps_ref, jac_ref, res_ref, pid_ref, hot_ref, place_ref, turned_ref, step_ref, grad_ref, right_ref, left_ref
+    steps_ref, jac_ref, res_ref, pid_ref, hot_ref, place_ref, turned_ref, step_ref, grad_ref, right_ref, left_ref, table_ref
 ):
-    blocks = [steps_ref[k * LOWS : (k + 1) * LOWS, 0, :] for k in range(4)]
-    first = low_lanes((LOWS, 128))
-    rows = []
-    for axis in range(3):
-        halves = []
-        for kk in range(2):
-            at = (axis // 2) * 128
-            one, two = blocks[2 * kk][:, at : at + 128], blocks[2 * kk + 1][:, at : at + 128]
-            if axis % 2:
-                halves.append(jnp.where(first, swap_halves(one), two))
-            else:
-                halves.append(jnp.where(first, one, swap_halves(two)))
-        rows.append(jnp.concatenate(halves, axis=1))
     for axis in range(3):
         for low in range(LOWS):
-            step_ref[axis : axis + 1, low * HIGHS : (low + 1) * HIGHS] = rows[axis][low : low + 1, :]
-    table = jnp.concatenate(rows, axis=0)
+            at = axis * OWNED + (low % 2) * HIGHS
+            row = steps_ref[low // 2, :, at : at + HIGHS]
+            table_ref[axis * LOWS + low : axis * LOWS + low + 1, :] = row
+            step_ref[axis : axis + 1, low * HIGHS : (low + 1) * HIGHS] = row
+    table = table_ref[...]
     top, rest = split(table)
     table = jnp.concatenate([top, rest], axis=0).astype(BF16)
     found = jnp.dot(table, hot_ref[...], preferred_element_type=F32)
@@ -195,13 +173,25 @@
     cams = cam_ids.reshape(count // 128, 128)
     parts = pl.pallas_call(
         stats_kernel,
-        out_shape=shape((OWNERS, 1, 640)),
+        out_shape=shape((OWNERS, 1, 9 * OWNED)),
         in_specs=[vmem] * 3,
         out_specs=vmem,
         scratch_shapes=[pltpu.VMEM((HIGHS, count), BF16), pltpu.VMEM((18 * LOWS, count), BF16)],
         name="stats",
     )(jac_point, resid, pids)
-    parts = exchange(parts, IMG_GROUPS)
+    parts = exchange(parts, CLOSE_GROUPS)
+    parts, pids, cams, owner_slot, jac_cam, damping = lax.optimization_barrier(
+        (parts, pids, cams, owner_slot, jac_cam, damping)
+    )
+    parts = pl.pallas_call(
+        gather_kernel,
+        out_shape=shape((OWNERS, 1, 9 * OWNED)),
+        in_specs=[vmem],
+        out_specs=vmem,
+        compiler_params=LIMIT,
+        name="gather",
+    )(parts)
+    arrived = exchange(parts, LINE_GROUPS)
     hot, place, turned = pl.pallas_call(
         prepare_kernel,
         out_shape=(shape((HIGHS, count), BF16), shape((1, count), jnp.int32), shape((2 * CAMP, count), BF16)),
@@ -211,21 +201,22 @@
         compiler_params=LIMIT,
         name="prepare",
     )(pids, cams, owner_slot.reshape(8, groups // 8), jac_cam)
+    arrived, hot, place, turned = lax.optimization_barrier((arrived, hot, place, turned))
     steps = pl.pallas_call(
         solve_kernel,
-        out_shape=shape((OWNERS, 1, 256)),
+        out_shape=shape((OWNERS, 1, 3 * OWNED)),
         in_specs=[vmem, vmem],
         out_specs=vmem,
         compiler_params=LIMIT,
         name="solve",
-    )(damping.reshape(1, 1), parts)
-    steps = exchange(steps, IMG_GROUPS)
+    )(damping.reshape(1, 1), arrived)
+    steps = exchange(steps, CLOSE_GROUPS)
     step, partial_grad = pl.pallas_call(
         camera_kernel,
         out_shape=(shape((3, points)), shape((groups, CAMP))),
         in_specs=[vmem] * 7,
         out_specs=(vmem, vmem),
-        scratch_shapes=[pltpu.VMEM((2 * CAMP, count), BF16), pltpu.VMEM((256, count), BF16)],
+        scratch_shapes=[pltpu.VMEM((2 * CAMP, count), BF16), pltpu.VMEM((256, count), BF16), pltpu.VMEM((3 * LOWS, HIGHS), F32)],
         compiler_params=LIMIT,
         name="camera",
     )(steps, jac_point, resid, pids, hot, place, turned)

time: 86.6 us -> 80.6 us (0.931)
  starting transfers between devices: 38.6 us -> 17.6 us
  blocking collectives: 31.5 us -> 51.2 us
  waiting for transfers between devices: 7.19 us -> 3.64 us
  local copies, waits for them, and re-layouts: 1.24 us -> 0.03 us
    all_to_all x2 -> x1, starting transfers between devices: 38.6 us -> 17.6 us  [exchange(): lax.all_to_all(value, FLAT, 0, 0, axis_index_groups=groups, tiled=True)]
    all_to_all x2 -> x4, blocking collectives: 31.5 us -> 51.2 us  [exchange(): lax.all_to_all(value, FLAT, 0, 0, axis_index_groups=groups, tiled=True)]
    all_to_all x2 -> x1, waiting for transfers between devices: 7.19 us -> 3.64 us  [exchange(): lax.all_to_all(value, FLAT, 0, 0, axis_index_groups=groups, tiled=True)]
    unnamed x12, local copies, waits for them, and re-layouts: 1.24 us -> 0.03 us
    pallas_call x2 -> x3, Pallas kernels: 3.09 us -> 2.95 us  [the longest x1 2.18 us: per_device(): pl.pallas_call(stats_kernel, out_shape=shape((OWNERS, 1, 9 * OWNED)), in_...]
  transfers between devices with their start and end apart: 2 -> 1, of which waited for: 2 -> 1; matrix products, arithmetic and copies ran while one was open for 0% -> 0% of each run, Pallas kernels for 1% -> 1%
where the time goes in v4:
time: 80.6 us; the launch traced here: 80.1 us
  blocking collectives  51.2 us (64%)
  starting transfers between devices  17.6 us (22%)
  Pallas kernels  5.58 us (7%)
  waiting for transfers between devices  3.64 us (5%)
  between operations  1.36 us (2%)
    all_to_all x4, blocking collectives, exchange(): lax.all_to_all(value, FLAT, 0, 0, axis_index_groups=groups, tiled=True)  51.2 us
    all_to_all x1, starting transfers between devices, exchange(): lax.all_to_all(value, FLAT, 0, 0, axis_index_groups=groups, tiled=True)  17.6 us
    all_to_all x1, waiting for transfers between devices, exchange(): lax.all_to_all(value, FLAT, 0, 0, axis_index_groups=groups, tiled=True)  3.64 us
    pallas_call x1, Pallas kernels, per_device(): pl.pallas_call(stats_kernel, out_shape=shape((OWNERS, 1, 9 * OWNED)), in_...  2.18 us
    pallas_call x1, Pallas kernels, per_device(): pl.pallas_call(camera_kernel, out_shape=(shape((3, points)), shape((group...  1.9 us
  transfers between devices with their start and end apart: 1, of which 1 were waited for; matrix products, arithmetic and copies ran while one was open for 0% of the time, Pallas kernels for 1%

profile of v4, /device:TPU:1, one launch (start us, length us, event | category | flops | bytes accessed | tf_op | source)
XLA Modules:
  0.0 80.1 jit_solution(13815776363104579881)
XLA Ops:
  0.6 0.0 copy-start
  0.6 2.2 %stats.1 = f32[8,1,4608]{2,1,0:T(1,128)} custom-call(f32[6,2048]{1,0:T(8,128)} %jac_ref.4, f32[2,2048]{1,0:T(2,128)} %res_ref.3, s32[16,128]{1,0:T(8,128)} %bitcast.8), custom_call_target="tpu_custom_call" | custom-call | tf_op jit(solution)/shard_map/stats/pallas_call | solution.py:174
  2.8 10.5 %all_to_all.25.parts_ref = f32[8,1,4608]{2,1,0:T(1,128)S(1)} all-to-all(f32[8,1,4608]{2,1,0:T(1,128)} %stats.1), channel_id=1, replica_groups={{324,332,452,460,68,76,196,204},{325,333,453,461,69,77,197,205},{326,33..., dimensions={0} | all-to-all | bytes 294912 | tf_op jit(solution)/shard_map/all_to_all | solution.py:164
  13.3 0.7 gather.1
  14.0 0.0 copy-start.2
  14.0 0.0 copy-start.4
  14.0 0.0 copy-start.5
  14.0 17.6 %all-to-all-start.1 = ((f32[8,1,4608]{2,1,0:T(1,128)}), f32[8,1,4608]{2,1,0:T(1,128)S(1)}, u32[]{:S(2)}, u32[]{:S(2)}) async-start(f32[8,1,4608]{2,1,0:T(1,128)} %gather.1), calls=%async_computation.1 | async-start | bytes 294912 | tf_op jit(solution)/shard_map/all_to_all | solution.py:164
  32.2 0.0 copy-done
  32.2 0.0 copy-done.2
  32.3 0.0 copy-done.4
  32.3 0.0 copy-done.5
  32.3 0.7 prepare.1
  33.0 3.6 %all-to-all-done.1.parts_ref = f32[8,1,4608]{2,1,0:T(1,128)S(1)} async-done(((f32[8,1,4608]{2,1,0:T(1,128)}), f32[8,1,4608]{2,1,0:T(1,128)S(1)}, u32[]{:S(2)}, u32[]{:S(2)}) %all-to-all-start.1) | async-done | bytes 147488 | tf_op jit(solution)/shard_map/all_to_all | solution.py:164
  36.7 0.1 solve.1
  36.8 0.0 copy-start.1
  36.8 0.0 copy-start.3
  36.8 9.2 %all_to_all.26.steps_ref = f32[8,1,1536]{2,1,0:T(1,128)S(1)} all-to-all(f32[8,1,1536]{2,1,0:T(1,128)S(1)} %solve.1), channel_id=1, replica_groups={{324,332,452,460,68,76,196,204},{325,333,453,461,69,77,197,205},{326,33..., dimensions={0} | all-to-all | bytes 98304 | tf_op jit(solution)/shard_map/all_to_all | solution.py:164
  45.9 0.0 copy-done.1
  45.9 0.0 copy-done.3
  45.9 1.9 %camera.1 = (f32[3,4096]{1,0:T(4,128)}, f32[1024,128]{1,0:T(8,128)S(1)}) custom-call(f32[8,1,1536]{2,1,0:T(1,128)S(1)} %all_to_all.26.steps_ref, f32[6,2048]{1,0:T(8,128)S(1)} %copy-done.1, f32[2,2048]{1,0:T(2,128)S(1)} %copy-done.3, s32[16,128]{1,0:T(8,128)S(1)} %bitcast.10, bf16[256,2048]{1,0:T(8,128)(2,1)S(1)} %get-tuple-element.27.hot_ref, ...), custom_call_target="tpu_custom_call" | custom-call | tf_op jit(solution)/shard_map/camera/pallas_call | solution.py:214
  47.8 18.3 %all_to_all.27 = f32[32,32,128]{2,1,0:T(8,128)S(1)} all-to-all(f32[32,32,128]{2,1,0:T(8,128)S(1)} %bitcast.7), channel_id=1, replica_groups={{324,325,326,327,320,321,322,323,452,453,454,455,448,449,450,451,68,69,..., dimensions={0} | all-to-all | bytes 1048576 | tf_op jit(solution)/shard_map/all_to_all | solution.py:164
  66.2 13.3 %all_to_all.28 = f32[16,2,128]{2,1,0:T(2,128)S(1)} all-to-all(f32[16,2,128]{2,1,0:T(2,128)S(1)} %bitcast.13), channel_id=1, replica_groups={{324,332,340,348,356,364,372,380,260,268,276,284,292,300,308,316},{325,..., dimensions={0} | all-to-all | bytes 32768 | tf_op jit(solution)/shard_map/all_to_all | solution.py:164
  79.5 0.6 reduce_sum.19
  (1 shorter events, 0.0 us)
Async XLA Ops:
  0.6 31.6 %copy-start = (bf16[2048,256]{1,0:T(8,128)(2,1)S(1)}, bf16[2048,256]{1,0:T(8,128)(2,1)}, u32[]{:S(2)}) copy-start(bf16[2048,256]{1,0:T(8,128)(2,1)} %jac_ref.3) | copy-start | bytes 3145732
  14.0 18.3 %copy-start.2 = (s32[2048]{0:T(1024)S(1)}, s32[2048]{0:T(1024)}, u32[]{:S(2)}) copy-start(s32[2048]{0:T(1024)} %param.10) | copy-start | bytes 24580
  14.0 18.3 %copy-start.4 = (s32[2048]{0:T(1024)S(1)}, s32[2048]{0:T(1024)}, u32[]{:S(2)}) copy-start(s32[2048]{0:T(1024)} %param.11) | copy-start | bytes 24580
  14.0 18.3 %copy-start.5 = (s32[1024]{0:T(1024)S(1)}, s32[1024]{0:T(1024)}, u32[]{:S(2)}) copy-start(s32[1024]{0:T(1024)} %param.12) | copy-start | bytes 12292
  14.0 22.7 %all-to-all-start.1 = ((f32[8,1,4608]{2,1,0:T(1,128)}), f32[8,1,4608]{2,1,0:T(1,128)S(1)}, u32[]{:S(2)}, u32[]{:S(2)}) async-start(f32[8,1,4608]{2,1,0:T(1,128)} %gather.1), calls=%async_computation.1 | async-start | bytes 294912 | tf_op jit(solution)/shard_map/all_to_all | solution.py:164
  36.8 9.2 %copy-start.1 = (f32[6,2048]{1,0:T(8,128)S(1)}, f32[6,2048]{1,0:T(8,128)}, u32[]{:S(2)}) copy-start(f32[6,2048]{1,0:T(8,128)} %jac_ref.4) | copy-start | bytes 147460
  36.8 9.2 %copy-start.3 = (f32[2,2048]{1,0:T(2,128)S(1)}, f32[2,2048]{1,0:T(2,128)}, u32[]{:S(2)}) copy-start(f32[2,2048]{1,0:T(2,128)} %res_ref.3) | copy-start | bytes 49156

commit v5 on v4

--- a/solution.py
+++ b/solution.py
@@ -39,8 +39,9 @@
 
 
 def one_hot(row, count):
-    index = lax.broadcasted_iota(jnp.int32, (count, row.shape[1]), 0)
-    return jnp.where(index == row, 1.0, 0.0).astype(BF16)
+    index = lax.broadcasted_iota(jnp.int32, (count, row.shape[1]), 0).astype(F32).astype(BF16)
+    row = jnp.clip(row, -1, 256).astype(F32).astype(BF16)
+    return jnp.where(index == row, jnp.ones((), BF16), jnp.zeros((), BF16))
 
 
 def stats_kernel(jac_ref, res_ref, pid_ref, out_ref, hot_ref, terms_ref):
@@ -88,14 +89,15 @@
     return total
 
 
-def gather_kernel(parts_ref, out_ref):
+def gather_kernel(damp_ref, parts_ref, out_ref, factor_ref):
     out_ref[...] = jnp.broadcast_to(total_of(parts_ref)[None], out_ref.shape)
-
-
-def solve_kernel(damp_ref, parts_ref, out_ref):
+    factor_ref[...] = jnp.broadcast_to(damp_ref[...], factor_ref.shape)
+
+
+def solve_kernel(factor_ref, parts_ref, out_ref):
     total = total_of(parts_ref)
     s = [total[:, v * OWNED : (v + 1) * OWNED] for v in range(9)]
-    factor = damp_ref[...]
+    factor = factor_ref[...]
     h01, h02, h12 = s[1], s[2], s[4]
     a00 = s[0] + factor * (s[0] + 1.0)
     a11 = s[3] + factor * (s[3] + 1.0)
@@ -180,18 +182,6 @@
         name="stats",
     )(jac_point, resid, pids)
     parts = exchange(parts, CLOSE_GROUPS)
-    parts, pids, cams, owner_slot, jac_cam, damping = lax.optimization_barrier(
-        (parts, pids, cams, owner_slot, jac_cam, damping)
-    )
-    parts = pl.pallas_call(
-        gather_kernel,
-        out_shape=shape((OWNERS, 1, 9 * OWNED)),
-        in_specs=[vmem],
-        out_specs=vmem,
-        compiler_params=LIMIT,
-        name="gather",
-    )(parts)
-    arrived = exchange(parts, LINE_GROUPS)
     hot, place, turned = pl.pallas_call(
         prepare_kernel,
         out_shape=(shape((HIGHS, count), BF16), shape((1, count), jnp.int32), shape((2 * CAMP, count), BF16)),
@@ -201,7 +191,16 @@
         compiler_params=LIMIT,
         name="prepare",
     )(pids, cams, owner_slot.reshape(8, groups // 8), jac_cam)
-    arrived, hot, place, turned = lax.optimization_barrier((arrived, hot, place, turned))
+    parts, hot, place, turned = lax.optimization_barrier((parts, hot, place, turned))
+    parts, factor = pl.pallas_call(
+        gather_kernel,
+        out_shape=(shape((OWNERS, 1, 9 * OWNED)), shape((1, OWNED))),
+        in_specs=[vmem] * 2,
+        out_specs=(vmem, vmem),
+        compiler_params=LIMIT,
+        name="gather",
+    )(damping.reshape(1, 1), parts)
+    arrived = exchange(parts, LINE_GROUPS)
     steps = pl.pallas_call(
         solve_kernel,
         out_shape=shape((OWNERS, 1, 3 * OWNED)),
@@ -209,7 +208,7 @@
         out_specs=vmem,
         compiler_params=LIMIT,
         name="solve",
-    )(damping.reshape(1, 1), arrived)
+    )(factor, arrived)
     steps = exchange(steps, CLOSE_GROUPS)
     step, partial_grad = pl.pallas_call(
         camera_kernel,

time: 80.6 us -> 79.6 us (0.988)
  blocking collectives: 51.2 us -> 63.1 us
  starting transfers between devices: 17.6 us -> 7.49 us
  waiting for transfers between devices: 3.64 us -> 0.75 us
  local copies, waits for them, and re-layouts: 0.03 us -> 1.24 us
  Pallas kernels: 5.58 us -> 4.45 us
    all_to_all x4, blocking collectives: 51.2 us -> 63.1 us  [exchange(): lax.all_to_all(value, FLAT, 0, 0, axis_index_groups=groups, tiled=True)]
    all_to_all x1, starting transfers between devices: 17.6 us -> 7.49 us  [exchange(): lax.all_to_all(value, FLAT, 0, 0, axis_index_groups=groups, tiled=True)]
    all_to_all x1, waiting for transfers between devices: 3.64 us -> 0.75 us  [exchange(): lax.all_to_all(value, FLAT, 0, 0, axis_index_groups=groups, tiled=True)]
    unnamed x12, local copies, waits for them, and re-layouts: 0.03 us -> 1.24 us
where the time goes in v5:
time: 79.6 us; the launch traced here: 79.1 us
  blocking collectives  63.1 us (79%)
  starting transfers between devices  7.49 us (9%)
  Pallas kernels  4.45 us (6%)
  between operations  1.36 us (2%)
  local copies, waits for them, and re-layouts  1.24 us (2%)
    all_to_all x4, blocking collectives, exchange(): lax.all_to_all(value, FLAT, 0, 0, axis_index_groups=groups, tiled=True)  63.1 us
    all_to_all x1, starting transfers between devices, exchange(): lax.all_to_all(value, FLAT, 0, 0, axis_index_groups=groups, tiled=True)  7.49 us
    pallas_call x1, Pallas kernels, per_device(): pl.pallas_call(stats_kernel, out_shape=shape((OWNERS, 1, 9 * OWNED)), in_...  2.09 us
    pallas_call x1, Pallas kernels, per_device(): pl.pallas_call(camera_kernel, out_shape=(shape((3, points)), shape((group...  1.81 us
  transfers between devices with their start and end apart: 1, of which 1 were waited for; matrix products, arithmetic and copies ran while one was open for 0% of the time, Pallas kernels for 1%

profile of v5, /device:TPU:1, one launch (start us, length us, event | category | flops | bytes accessed | tf_op | source)
XLA Modules:
  0.0 79.1 jit_solution(15672218414635627318)
XLA Ops:
  0.6 2.1 %stats.1 = f32[8,1,4608]{2,1,0:T(1,128)} custom-call(f32[6,2048]{1,0:T(8,128)} %jac_ref.5, f32[2,2048]{1,0:T(2,128)} %res_ref.3, s32[16,128]{1,0:T(8,128)} %bitcast.8), custom_call_target="tpu_custom_call" | custom-call | tf_op jit(solution)/shard_map/stats/pallas_call | solution.py:176
  2.7 0.0 copy-start.2
  2.7 0.0 copy-start.4
  2.7 7.5 %all-to-all-start = ((f32[8,1,4608]{2,1,0:T(1,128)}), f32[8,1,4608]{2,1,0:T(1,128)S(1)}, u32[]{:S(2)}, u32[]{:S(2)}) async-start(f32[8,1,4608]{2,1,0:T(1,128)} %stats.1), calls=%async_computation | async-start | bytes 294912 | tf_op jit(solution)/shard_map/all_to_all | solution.py:166
  10.2 0.0 copy-start.5
  10.9 0.0 copy-done.2
  10.9 0.0 copy-done.4
  10.9 0.0 copy-done.5
  10.9 0.0 copy-start
  10.9 1.2 %copy-done = bf16[2048,256]{1,0:T(8,128)(2,1)S(1)} copy-done((bf16[2048,256]{1,0:T(8,128)(2,1)S(1)}, bf16[2048,256]{1,0:T(8,128)(2,1)}, u32[]{:S(2)}) %copy-start) | copy-done | bytes 1048600
  12.1 0.4 prepare.1
  12.6 0.8 all-to-all-done.parts_ref
  13.3 0.1 gather.1
  13.4 22.3 %all_to_all.25.parts_ref = f32[8,1,4608]{2,1,0:T(1,128)S(1)} all-to-all(f32[8,1,4608]{2,1,0:T(1,128)S(1)} %get-tuple-element.18), channel_id=1, replica_groups={{324,340,356,372,260,276,292,308},{325,341,357,373,261,277,293,309},{32..., dimensions={0} | all-to-all | bytes 294912 | tf_op jit(solution)/shard_map/all_to_all | solution.py:166
  35.8 0.0 copy-start.1
  35.8 0.0 copy-start.3
  35.8 9.2 %all_to_all.26.steps_ref = f32[8,1,1536]{2,1,0:T(1,128)S(1)} all-to-all(f32[8,1,1536]{2,1,0:T(1,128)S(1)} %solve.1), channel_id=1, replica_groups={{324,332,452,460,68,76,196,204},{325,333,453,461,69,77,197,205},{326,33..., dimensions={0} | all-to-all | bytes 98304 | tf_op jit(solution)/shard_map/all_to_all | solution.py:166
  45.0 0.0 copy-done.1
  45.0 0.0 copy-done.3
  45.0 1.8 %camera.1 = (f32[3,4096]{1,0:T(4,128)}, f32[1024,128]{1,0:T(8,128)S(1)}) custom-call(f32[8,1,1536]{2,1,0:T(1,128)S(1)} %all_to_all.26.steps_ref, f32[6,2048]{1,0:T(8,128)S(1)} %copy-done.1, f32[2,2048]{1,0:T(2,128)S(1)} %copy-done.3, s32[16,128]{1,0:T(8,128)S(1)} %bitcast.10, bf16[256,2048]{1,0:T(8,128)(2,1)S(1)} %get-tuple-element.19.hot_ref, ...), custom_call_target="tpu_custom_call" | custom-call | tf_op jit(solution)/shard_map/camera/pallas_call | solution.py:213
  46.8 18.3 %all_to_all.27 = f32[32,32,128]{2,1,0:T(8,128)S(1)} all-to-all(f32[32,32,128]{2,1,0:T(8,128)S(1)} %bitcast.7), channel_id=1, replica_groups={{324,325,326,327,320,321,322,323,452,453,454,455,448,449,450,451,68,69,..., dimensions={0} | all-to-all | bytes 1048576 | tf_op jit(solution)/shard_map/all_to_all | solution.py:166
  65.2 13.3 %all_to_all.28 = f32[16,2,128]{2,1,0:T(2,128)S(1)} all-to-all(f32[16,2,128]{2,1,0:T(2,128)S(1)} %bitcast.13), channel_id=1, replica_groups={{324,332,340,348,356,364,372,380,260,268,276,284,292,300,308,316},{325,..., dimensions={0} | all-to-all | bytes 32768 | tf_op jit(solution)/shard_map/all_to_all | solution.py:166
  78.5 0.6 reduce_sum.19
  (2 shorter events, 0.1 us)
Async XLA Ops:
  2.7 8.2 %copy-start.2 = (s32[2048]{0:T(1024)S(1)}, s32[2048]{0:T(1024)}, u32[]{:S(2)}) copy-start(s32[2048]{0:T(1024)} %param.10) | copy-start | bytes 24580
  2.7 8.2 %copy-start.4 = (s32[2048]{0:T(1024)S(1)}, s32[2048]{0:T(1024)}, u32[]{:S(2)}) copy-start(s32[2048]{0:T(1024)} %param.11) | copy-start | bytes 24580
  2.7 10.6 %all-to-all-start = ((f32[8,1,4608]{2,1,0:T(1,128)}), f32[8,1,4608]{2,1,0:T(1,128)S(1)}, u32[]{:S(2)}, u32[]{:S(2)}) async-start(f32[8,1,4608]{2,1,0:T(1,128)} %stats.1), calls=%async_computation | async-start | bytes 294912 | tf_op jit(solution)/shard_map/all_to_all | solution.py:166
  10.2 0.7 copy-start.5
  10.9 1.2 %copy-start = (bf16[2048,256]{1,0:T(8,128)(2,1)S(1)}, bf16[2048,256]{1,0:T(8,128)(2,1)}, u32[]{:S(2)}) copy-start(bf16[2048,256]{1,0:T(8,128)(2,1)} %jac_ref.4) | copy-start | bytes 3145732
  35.8 9.2 %copy-start.1 = (f32[6,2048]{1,0:T(8,128)S(1)}, f32[6,2048]{1,0:T(8,128)}, u32[]{:S(2)}) copy-start(f32[6,2048]{1,0:T(8,128)} %jac_ref.5) | copy-start | bytes 147460
  35.8 9.2 %copy-start.3 = (f32[2,2048]{1,0:T(2,128)S(1)}, f32[2,2048]{1,0:T(2,128)}, u32[]{:S(2)}) copy-start(f32[2,2048]{1,0:T(2,128)} %res_ref.3) | copy-start | bytes 49156

commit v6 on v5

--- a/solution.py
+++ b/solution.py
@@ -13,9 +13,9 @@
 ALL = ("y", "z", "x", "c")
 FLAT = ("img", "lm")
 GRID = np.arange(512).reshape(4, 16, 4, 2)
-TURNED = GRID[[2, 3, 0, 1]][:, [z ^ 8 for z in range(16)]][:, :, [2, 3, 0, 1]]
+TURNED = GRID[[2, 3, 0, 1]][:, [z ^ 8 for z in range(16)]][:, :, [2, 3, 0, 1], ::-1]
 PAIRS = TURNED.reshape(4, 8, 2, 4, 2)
-CLOSE_GROUPS = [PAIRS[:, z, :, x, c].reshape(-1).tolist() for z in range(8) for x in range(4) for c in range(2)]
+CLOSE_GROUPS = [PAIRS[:, z, :, x, c].T.reshape(-1).tolist() for z in range(8) for x in range(4) for c in range(2)]
 LINE_GROUPS = [PAIRS[y, :, z, x, c].tolist() for y in range(4) for z in range(2) for x in range(4) for c in range(2)]
 NEAR_GROUPS = [TURNED[:, z].reshape(-1).tolist() for z in range(16)]
 FAR_GROUPS = [TURNED[y, :, x, c].tolist() for y in range(4) for x in range(4) for c in range(2)]
@@ -72,7 +72,7 @@
     cam = row_of(cam_ref)
     hot = one_hot(cam & 127, 128)
     slot = slot_ref[...]
-    y, z, x = (slot >> 8) ^ 2, ((slot >> 4) & 15) ^ 8, ((slot >> 1) & 7) ^ 4
+    y, z, x = (slot >> 8) ^ 2, ((slot >> 4) & 15) ^ 8, ((slot >> 1) & 7) ^ 5
     above, below = y * 8 + x, z * 2 + (slot & 1)
     table = jnp.concatenate([above, below], axis=0).astype(F32).astype(BF16)
     found = jnp.dot(table, hot, preferred_element_type=F32)
@@ -146,9 +146,9 @@
     right_ref[CAMP:, :] = rest.astype(BF16)
     place = place_ref[...]
     for q in range(grad_ref.shape[0] // 256):
-        left_ref[...] = one_hot(place - q * 256, 256)
-        both = lax.dot_general(left_ref[...], right_ref[...], NT, preferred_element_type=F32)
-        grad_ref[q * 256 : (q + 1) * 256, :] = both[:, :CAMP] + both[:, CAMP:]
+        left_ref[q * 256 : (q + 1) * 256, :] = one_hot(place - q * 256, 256)
+    both = lax.dot_general(left_ref[...], right_ref[...], NT, preferred_element_type=F32)
+    grad_ref[...] = both[:, :CAMP] + both[:, CAMP:]
 
 
 def shape(dims, kind=F32):
@@ -215,7 +215,7 @@
         out_shape=(shape((3, points)), shape((groups, CAMP))),
         in_specs=[vmem] * 7,
         out_specs=(vmem, vmem),
-        scratch_shapes=[pltpu.VMEM((2 * CAMP, count), BF16), pltpu.VMEM((256, count), BF16), pltpu.VMEM((3 * LOWS, HIGHS), F32)],
+        scratch_shapes=[pltpu.VMEM((2 * CAMP, count), BF16), pltpu.VMEM((groups, count), BF16), pltpu.VMEM((3 * LOWS, HIGHS), F32)],
         compiler_params=LIMIT,
         name="camera",
     )(steps, jac_point, resid, pids, hot, place, turned)

time: 79.6 us -> 78.8 us (0.990)
  no operation moved by 1% of the time
where the time goes in v6:
time: 78.8 us; the launch traced here: 78.3 us
  blocking collectives  62.5 us (79%)
  starting transfers between devices  7.49 us (10%)
  Pallas kernels  4.3 us (5%)
  between operations  1.37 us (2%)
  local copies, waits for them, and re-layouts  1.24 us (2%)
    all_to_all x4, blocking collectives, exchange(): lax.all_to_all(value, FLAT, 0, 0, axis_index_groups=groups, tiled=True)  62.5 us
    all_to_all x1, starting transfers between devices, exchange(): lax.all_to_all(value, FLAT, 0, 0, axis_index_groups=groups, tiled=True)  7.49 us
    pallas_call x1, Pallas kernels, per_device(): pl.pallas_call(stats_kernel, out_shape=shape((OWNERS, 1, 9 * OWNED)), in_...  2.09 us
    pallas_call x1, Pallas kernels, per_device(): pl.pallas_call(camera_kernel, out_shape=(shape((3, points)), shape((group...  1.66 us
  transfers between devices with their start and end apart: 1, of which 1 were waited for; matrix products, arithmetic and copies ran while one was open for 0% of the time, Pallas kernels for 1%

profile of v6, /device:TPU:1, one launch (start us, length us, event | category | flops | bytes accessed | tf_op | source)
XLA Modules:
  0.0 78.3 jit_solution(13902947747337013373)
XLA Ops:
  0.6 2.1 %stats.1 = f32[8,1,4608]{2,1,0:T(1,128)} custom-call(f32[6,2048]{1,0:T(8,128)} %jac_ref.5, f32[2,2048]{1,0:T(2,128)} %res_ref.3, s32[16,128]{1,0:T(8,128)} %bitcast.8), custom_call_target="tpu_custom_call" | custom-call | tf_op jit(solution)/shard_map/stats/pallas_call | solution.py:176
  2.7 0.0 copy-start.2
  2.7 0.0 copy-start.4
  2.7 7.5 %all-to-all-start = ((f32[8,1,4608]{2,1,0:T(1,128)}), f32[8,1,4608]{2,1,0:T(1,128)S(1)}, u32[]{:S(2)}, u32[]{:S(2)}) async-start(f32[8,1,4608]{2,1,0:T(1,128)} %stats.1), calls=%async_computation | async-start | bytes 294912 | tf_op jit(solution)/shard_map/all_to_all | solution.py:166
  10.2 0.0 copy-start.5
  10.9 0.0 copy-done.2
  10.9 0.0 copy-done.4
  10.9 0.0 copy-done.5
  10.9 0.0 copy-start
  10.9 1.2 %copy-done = bf16[2048,256]{1,0:T(8,128)(2,1)S(1)} copy-done((bf16[2048,256]{1,0:T(8,128)(2,1)S(1)}, bf16[2048,256]{1,0:T(8,128)(2,1)}, u32[]{:S(2)}) %copy-start) | copy-done | bytes 1048600
  12.1 0.4 prepare.1
  12.6 0.8 all-to-all-done.parts_ref
  13.3 0.1 gather.1
  13.4 24.3 %all_to_all.25.parts_ref = f32[8,1,4608]{2,1,0:T(1,128)S(1)} all-to-all(f32[8,1,4608]{2,1,0:T(1,128)S(1)} %get-tuple-element.18), channel_id=1, replica_groups={{325,341,357,373,261,277,293,309},{324,340,356,372,260,276,292,308},{32..., dimensions={0} | all-to-all | bytes 294912 | tf_op jit(solution)/shard_map/all_to_all | solution.py:166
  37.8 0.0 copy-start.1
  37.8 0.0 copy-start.3
  37.8 6.9 %all_to_all.26.steps_ref = f32[8,1,1536]{2,1,0:T(1,128)S(1)} all-to-all(f32[8,1,1536]{2,1,0:T(1,128)S(1)} %solve.1), channel_id=1, replica_groups={{325,453,69,197,333,461,77,205},{324,452,68,196,332,460,76,204},{327,45..., dimensions={0} | all-to-all | bytes 98304 | tf_op jit(solution)/shard_map/all_to_all | solution.py:166
  44.7 0.0 copy-done.1
  44.7 0.0 copy-done.3
  44.7 1.7 %camera.1 = (f32[3,4096]{1,0:T(4,128)}, f32[1024,128]{1,0:T(8,128)S(1)}) custom-call(f32[8,1,1536]{2,1,0:T(1,128)S(1)} %all_to_all.26.steps_ref, f32[6,2048]{1,0:T(8,128)S(1)} %copy-done.1, f32[2,2048]{1,0:T(2,128)S(1)} %copy-done.3, s32[16,128]{1,0:T(8,128)S(1)} %bitcast.10, bf16[256,2048]{1,0:T(8,128)(2,1)S(1)} %get-tuple-element.19.hot_ref, ...), custom_call_target="tpu_custom_call" | custom-call | tf_op jit(solution)/shard_map/camera/pallas_call | solution.py:213
  46.3 18.0 %all_to_all.27 = f32[32,32,128]{2,1,0:T(8,128)S(1)} all-to-all(f32[32,32,128]{2,1,0:T(8,128)S(1)} %bitcast.7), channel_id=1, replica_groups={{325,324,327,326,321,320,323,322,453,452,455,454,449,448,451,450,69,68,..., dimensions={0} | all-to-all | bytes 1048576 | tf_op jit(solution)/shard_map/all_to_all | solution.py:166
  64.4 13.3 %all_to_all.28 = f32[16,2,128]{2,1,0:T(2,128)S(1)} all-to-all(f32[16,2,128]{2,1,0:T(2,128)S(1)} %bitcast.13), channel_id=1, replica_groups={{325,333,341,349,357,365,373,381,261,269,277,285,293,301,309,317},{324,..., dimensions={0} | all-to-all | bytes 32768 | tf_op jit(solution)/shard_map/all_to_all | solution.py:166
  77.7 0.6 reduce_sum.19
  (2 shorter events, 0.1 us)
Async XLA Ops:
  2.7 8.2 %copy-start.2 = (s32[2048]{0:T(1024)S(1)}, s32[2048]{0:T(1024)}, u32[]{:S(2)}) copy-start(s32[2048]{0:T(1024)} %param.10) | copy-start | bytes 24580
  2.7 8.2 %copy-start.4 = (s32[2048]{0:T(1024)S(1)}, s32[2048]{0:T(1024)}, u32[]{:S(2)}) copy-start(s32[2048]{0:T(1024)} %param.11) | copy-start | bytes 24580
  2.7 10.6 %all-to-all-start = ((f32[8,1,4608]{2,1,0:T(1,128)}), f32[8,1,4608]{2,1,0:T(1,128)S(1)}, u32[]{:S(2)}, u32[]{:S(2)}) async-start(f32[8,1,4608]{2,1,0:T(1,128)} %stats.1), calls=%async_computation | async-start | bytes 294912 | tf_op jit(solution)/shard_map/all_to_all | solution.py:166
  10.2 0.7 copy-start.5
  10.9 1.2 %copy-start = (bf16[2048,256]{1,0:T(8,128)(2,1)S(1)}, bf16[2048,256]{1,0:T(8,128)(2,1)}, u32[]{:S(2)}) copy-start(bf16[2048,256]{1,0:T(8,128)(2,1)} %jac_ref.4) | copy-start | bytes 3145732
  37.8 6.9 %copy-start.1 = (f32[6,2048]{1,0:T(8,128)S(1)}, f32[6,2048]{1,0:T(8,128)}, u32[]{:S(2)}) copy-start(f32[6,2048]{1,0:T(8,128)} %jac_ref.5) | copy-start | bytes 147460
  37.8 6.9 %copy-start.3 = (f32[2,2048]{1,0:T(2,128)S(1)}, f32[2,2048]{1,0:T(2,128)}, u32[]{:S(2)}) copy-start(f32[2,2048]{1,0:T(2,128)} %res_ref.3) | copy-start | bytes 49156

commit v7 on v6

--- a/solution.py
+++ b/solution.py
@@ -13,7 +13,7 @@
 ALL = ("y", "z", "x", "c")
 FLAT = ("img", "lm")
 GRID = np.arange(512).reshape(4, 16, 4, 2)
-TURNED = GRID[[2, 3, 0, 1]][:, [z ^ 8 for z in range(16)]][:, :, [2, 3, 0, 1], ::-1]
+TURNED = GRID[[2, 3, 0, 1]][:, [(z + 10) % 16 for z in range(16)]][:, :, [2, 3, 0, 1], ::-1]
 PAIRS = TURNED.reshape(4, 8, 2, 4, 2)
 CLOSE_GROUPS = [PAIRS[:, z, :, x, c].T.reshape(-1).tolist() for z in range(8) for x in range(4) for c in range(2)]
 LINE_GROUPS = [PAIRS[y, :, z, x, c].tolist() for y in range(4) for z in range(2) for x in range(4) for c in range(2)]
@@ -72,7 +72,7 @@
     cam = row_of(cam_ref)
     hot = one_hot(cam & 127, 128)
     slot = slot_ref[...]
-    y, z, x = (slot >> 8) ^ 2, ((slot >> 4) & 15) ^ 8, ((slot >> 1) & 7) ^ 5
+    y, z, x = ((slot >> 8) - 2) & 3, ((slot >> 4) - 10) & 15, ((slot >> 1) & 7) ^ 5
     above, below = y * 8 + x, z * 2 + (slot & 1)
     table = jnp.concatenate([above, below], axis=0).astype(F32).astype(BF16)
     found = jnp.dot(table, hot, preferred_element_type=F32)

time: 78.8 us -> 78.7 us (level)
  no operation moved by 1% of the time
where the time goes in v7:
time: 78.7 us; the launch traced here: 78.2 us
  blocking collectives  62.4 us (79%)
  starting transfers between devices  7.49 us (10%)
  Pallas kernels  4.31 us (5%)
  between operations  1.37 us (2%)
  local copies, waits for them, and re-layouts  1.24 us (2%)
    all_to_all x4, blocking collectives, exchange(): lax.all_to_all(value, FLAT, 0, 0, axis_index_groups=groups, tiled=True)  62.4 us
    all_to_all x1, starting transfers between devices, exchange(): lax.all_to_all(value, FLAT, 0, 0, axis_index_groups=groups, tiled=True)  7.49 us
    pallas_call x1, Pallas kernels, per_device(): pl.pallas_call(stats_kernel, out_shape=shape((OWNERS, 1, 9 * OWNED)), in_...  2.09 us
    pallas_call x1, Pallas kernels, per_device(): pl.pallas_call(camera_kernel, out_shape=(shape((3, points)), shape((group...  1.67 us
  transfers between devices with their start and end apart: 1, of which 1 were waited for; matrix products, arithmetic and copies ran while one was open for 0% of the time, Pallas kernels for 1%

profile of v7, /device:TPU:1, one launch (start us, length us, event | category | flops | bytes accessed | tf_op | source)
XLA Modules:
  0.0 78.2 jit_solution(8540038262530989097)
XLA Ops:
  0.6 2.1 %stats.1 = f32[8,1,4608]{2,1,0:T(1,128)} custom-call(f32[6,2048]{1,0:T(8,128)} %jac_ref.5, f32[2,2048]{1,0:T(2,128)} %res_ref.3, s32[16,128]{1,0:T(8,128)} %bitcast.8), custom_call_target="tpu_custom_call" | custom-call | tf_op jit(solution)/shard_map/stats/pallas_call | solution.py:176
  2.7 0.0 copy-start.2
  2.7 0.0 copy-start.4
  2.7 7.5 %all-to-all-start = ((f32[8,1,4608]{2,1,0:T(1,128)}), f32[8,1,4608]{2,1,0:T(1,128)S(1)}, u32[]{:S(2)}, u32[]{:S(2)}) async-start(f32[8,1,4608]{2,1,0:T(1,128)} %stats.1), calls=%async_computation | async-start | bytes 294912 | tf_op jit(solution)/shard_map/all_to_all | solution.py:166
  10.2 0.0 copy-start.5
  10.9 0.0 copy-done.2
  10.9 0.0 copy-done.4
  10.9 0.0 copy-done.5
  10.9 0.0 copy-start
  10.9 1.2 %copy-done = bf16[2048,256]{1,0:T(8,128)(2,1)S(1)} copy-done((bf16[2048,256]{1,0:T(8,128)(2,1)S(1)}, bf16[2048,256]{1,0:T(8,128)(2,1)}, u32[]{:S(2)}) %copy-start) | copy-done | bytes 1048600
  12.1 0.4 prepare.1
  12.6 0.7 all-to-all-done.parts_ref
  13.3 0.1 gather.1
  13.4 23.5 %all_to_all.25.parts_ref = f32[8,1,4608]{2,1,0:T(1,128)S(1)} all-to-all(f32[8,1,4608]{2,1,0:T(1,128)S(1)} %get-tuple-element.18), channel_id=1, replica_groups={{341,357,373,261,277,293,309,325},{340,356,372,260,276,292,308,324},{34..., dimensions={0} | all-to-all | bytes 294912 | tf_op jit(solution)/shard_map/all_to_all | solution.py:166
  37.0 0.0 copy-start.1
  37.0 0.0 copy-start.3
  37.0 7.3 %all_to_all.26.steps_ref = f32[8,1,1536]{2,1,0:T(1,128)S(1)} all-to-all(f32[8,1,1536]{2,1,0:T(1,128)S(1)} %solve.1), channel_id=1, replica_groups={{341,469,85,213,349,477,93,221},{340,468,84,212,348,476,92,220},{343,47..., dimensions={0} | all-to-all | bytes 98304 | tf_op jit(solution)/shard_map/all_to_all | solution.py:166
  44.3 0.0 copy-done.1
  44.3 0.0 copy-done.3
  44.3 1.7 %camera.1 = (f32[3,4096]{1,0:T(4,128)}, f32[1024,128]{1,0:T(8,128)S(1)}) custom-call(f32[8,1,1536]{2,1,0:T(1,128)S(1)} %all_to_all.26.steps_ref, f32[6,2048]{1,0:T(8,128)S(1)} %copy-done.1, f32[2,2048]{1,0:T(2,128)S(1)} %copy-done.3, s32[16,128]{1,0:T(8,128)S(1)} %bitcast.10, bf16[256,2048]{1,0:T(8,128)(2,1)S(1)} %get-tuple-element.19.hot_ref, ...), custom_call_target="tpu_custom_call" | custom-call | tf_op jit(solution)/shard_map/camera/pallas_call | solution.py:213
  45.9 17.9 %all_to_all.27 = f32[32,32,128]{2,1,0:T(8,128)S(1)} all-to-all(f32[32,32,128]{2,1,0:T(8,128)S(1)} %bitcast.7), channel_id=1, replica_groups={{341,340,343,342,337,336,339,338,469,468,471,470,465,464,467,466,85,84,..., dimensions={0} | all-to-all | bytes 1048576 | tf_op jit(solution)/shard_map/all_to_all | solution.py:166
  63.9 13.7 %all_to_all.28 = f32[16,2,128]{2,1,0:T(2,128)S(1)} all-to-all(f32[16,2,128]{2,1,0:T(2,128)S(1)} %bitcast.13), channel_id=1, replica_groups={{341,349,357,365,373,381,261,269,277,285,293,301,309,317,325,333},{340,..., dimensions={0} | all-to-all | bytes 32768 | tf_op jit(solution)/shard_map/all_to_all | solution.py:166
  77.6 0.6 reduce_sum.19
  (2 shorter events, 0.1 us)
Async XLA Ops:
  2.7 8.2 %copy-start.2 = (s32[2048]{0:T(1024)S(1)}, s32[2048]{0:T(1024)}, u32[]{:S(2)}) copy-start(s32[2048]{0:T(1024)} %param.10) | copy-start | bytes 24580
  2.7 8.2 %copy-start.4 = (s32[2048]{0:T(1024)S(1)}, s32[2048]{0:T(1024)}, u32[]{:S(2)}) copy-start(s32[2048]{0:T(1024)} %param.11) | copy-start | bytes 24580
  2.7 10.6 %all-to-all-start = ((f32[8,1,4608]{2,1,0:T(1,128)}), f32[8,1,4608]{2,1,0:T(1,128)S(1)}, u32[]{:S(2)}, u32[]{:S(2)}) async-start(f32[8,1,4608]{2,1,0:T(1,128)} %stats.1), calls=%async_computation | async-start | bytes 294912 | tf_op jit(solution)/shard_map/all_to_all | solution.py:166
  10.2 0.7 copy-start.5
  10.9 1.2 %copy-start = (bf16[2048,256]{1,0:T(8,128)(2,1)S(1)}, bf16[2048,256]{1,0:T(8,128)(2,1)}, u32[]{:S(2)}) copy-start(bf16[2048,256]{1,0:T(8,128)(2,1)} %jac_ref.4) | copy-start | bytes 3145732
  37.0 7.3 %copy-start.1 = (f32[6,2048]{1,0:T(8,128)S(1)}, f32[6,2048]{1,0:T(8,128)}, u32[]{:S(2)}) copy-start(f32[6,2048]{1,0:T(8,128)} %jac_ref.5) | copy-start | bytes 147460
  37.0 7.3 %copy-start.3 = (f32[2,2048]{1,0:T(2,128)S(1)}, f32[2,2048]{1,0:T(2,128)}, u32[]{:S(2)}) copy-start(f32[2,2048]{1,0:T(2,128)} %res_ref.3) | copy-start | bytes 49156
